TPU v7x, 32 devices: a whole 2x2x4 slice. The times are simulated.
32 devices in a mesh: seq: 16 (over z, y, core), ch: 2 (over x).
Axes of the slice: x: 2, y: 2, z: 4, core: 2. Of those that a mesh axis runs over, the one named last changes fastest.
Arguments:
- tokens: int32 [2, 32768], P(None, 'seq'), may hold values from 0 to 4
- embedding: bfloat16 [5, 256], replicated, may hold values from -6 to 6
- inner_weight: bfloat16 [256, 512], P(None, 'ch'), may hold values from -0.375 to 0.375
- gate_weight: bfloat16 [256, 512], P(None, 'ch'), may hold values from -0.375 to 0.375
- state_weight: bfloat16 [256, 32], replicated, may hold values from -0.375 to 0.375
- step_weight: bfloat16 [256, 8], P(None, 'ch'), may hold values from -0.375 to 0.375
- inner_kernel: float32 [4, 512], P(None, 'ch'), may hold values from -3 to 3
- state_kernel: float32 [4, 32], replicated, may hold values from -3 to 3
- step_bias: float32 [8], P('ch'), may hold values from -1 to 1
- decay_rates: float32 [8], P('ch'), may hold values from 3.0517578e-05 to 0.1
- skip_gain: float32 [8], P('ch'), may hold values from 0.1 to 18.5
- norm_gain: float32 [512], P('ch'), may hold values from 0.5 to 1.5
- out_weight: bfloat16 [512, 256], P('ch'), may hold values from -0.25 to 0.25
Outputs:
- mixed: bfloat16 [32768, 2, 256], P(('seq', 'ch'))
All inputs are finite; a program needn't handle non-finite values.
Results may differ from a plain program's by a relative error of at most 0.012.
Values may be sent and summed in bfloat16 or wider, within the bound.
A program may use at most 128 MiB of HBM per device.

v0:
```python
from functools import partial

import jax
import jax.numpy as jnp
from jax import lax
from jax.sharding import PartitionSpec as P

E = 512
BLOCK = 256


def shifted(value, axis, steps):
    count = lax.axis_size(axis)
    leading, last = (max(0, -steps), min(count, count - steps))
    return lax.ppermute(value, axis, [(source, source + steps) for source in range(leading, last)])


def prefix(x, axis, combine, identity):
    devices, index = (lax.axis_size(axis), lax.axis_index(axis))
    everything = jax.tree.map(lambda part: lax.all_gather(part, axis), x)
    start = jax.tree.map(
        lambda part, zero: jnp.broadcast_to(jnp.asarray(zero, part.dtype), part.shape), x, identity
    )

    def turn(k, before):
        reached = k < index
        new = combine(before, jax.tree.map(lambda part: part[k], everything))
        return jax.tree.map(lambda a, b: jnp.where(reached, a, b), new, before)

    return lax.fori_loop(0, devices, turn, start)


def from_partner(value, axis, stride):
    mask = 2**stride
    pairs = [(source, source ^ mask) for source in range(lax.axis_size(axis))]
    return lax.ppermute(value, axis, pairs)


def ssd_blocks(inner_rows, state_rows, step_sizes, decay_rates, skip_gain, block_rows):
    length, head_count = step_sizes.shape
    head_width = inner_rows.shape[-1] // head_count
    state_count = state_rows.shape[-1] // 2
    block_count = length // block_rows
    input_all = inner_rows.astype(jnp.float32).reshape(
        block_count, block_rows, head_count, head_width
    )
    key_all = (
        state_rows[:, :state_count]
        .astype(jnp.float32)
        .reshape(block_count, block_rows, state_count)
    )
    read_all = (
        state_rows[:, state_count:]
        .astype(jnp.float32)
        .reshape(block_count, block_rows, state_count)
    )
    step_all = step_sizes.reshape(block_count, block_rows, head_count)
    position = jnp.arange(block_rows)
    causal = (position[:, None] >= position[None, :])[:, :, None]

    def advance(carry_state, pieces):
        input_rows, key_rows, read_rows, step_rows = pieces
        log_decay = -step_rows * decay_rates[None, :]
        log_cumul = jnp.cumsum(log_decay, axis=0)
        read_key = jnp.dot(read_rows, key_rows.T, precision=lax.Precision.HIGHEST)
        spread = log_cumul[:, None, :] - log_cumul[None, :, :]
        kernel = (
            jnp.where(causal, jnp.exp(jnp.where(causal, spread, 0.0)), 0.0) * read_key[:, :, None]
        )
        driven = input_rows * step_rows[:, :, None]
        within = jnp.einsum("tsh,shp->thp", kernel, driven, precision=lax.Precision.HIGHEST)
        carried = jnp.exp(log_cumul)[:, :, None] * jnp.einsum(
            "tn,hpn->thp", read_rows, carry_state, precision=lax.Precision.HIGHEST
        )
        outputs = within + carried + skip_gain[None, :, None] * input_rows
        tail_decay = jnp.exp(log_cumul[-1][None, :] - log_cumul)
        new_state = jnp.exp(log_cumul[-1])[:, None, None] * carry_state + jnp.einsum(
            "sh,shp,sn->hpn", tail_decay, driven, key_rows, precision=lax.Precision.HIGHEST
        )
        return (new_state, outputs)

    zero_state = jnp.zeros((head_count, head_width, state_count), jnp.float32)
    final_state, outputs = lax.scan(advance, zero_state, (input_all, key_all, read_all, step_all))
    return (outputs.reshape(length, head_count * head_width), final_state)


def convolve(values, rim, kernel):
    extended = jnp.concatenate([rim, values], axis=-2).astype(jnp.float32)
    length = values.shape[-2]
    tap_count = kernel.shape[0]
    total = jnp.zeros(values.shape, jnp.float32)
    for offset in range(tap_count):
        begin = tap_count - 1 - offset
        total = total + kernel[offset] * extended[..., begin : begin + length, :]
    return jax.nn.silu(total).astype(jnp.bfloat16)


def project(strand_ids, embedding, inner_weight, gate_weight, state_weight, step_weight, step_bias):
    onehot = (strand_ids[:, :, None] == jnp.arange(embedding.shape[0])[None, None, :]).astype(
        jnp.bfloat16
    )
    embedded = jnp.einsum(
        "wrk,kd->wrd", onehot, embedding, preferred_element_type=jnp.float32
    ).astype(jnp.bfloat16)
    inner = jnp.einsum(
        "wrd,de->wre", embedded, inner_weight, preferred_element_type=jnp.float32
    ).astype(jnp.bfloat16)
    gate = jnp.einsum(
        "wrd,de->wre", embedded, gate_weight, preferred_element_type=jnp.float32
    ).astype(jnp.bfloat16)
    state_in = jnp.einsum(
        "wrd,de->wre", embedded, state_weight, preferred_element_type=jnp.float32
    ).astype(jnp.bfloat16)
    steps = jax.nn.softplus(
        jnp.einsum("wrd,dh->wrh", embedded, step_weight, preferred_element_type=jnp.float32)
        + step_bias
    )
    return (inner, gate, state_in, steps)


def combine_carry(earlier_part, later_part):
    total = earlier_part[0] + later_part[0]
    state = jnp.exp(later_part[0])[:, :, None, None] * earlier_part[1] + later_part[1]
    return (total, state)


def mixer(projected, inner_kernel, state_kernel, decay_rates, skip_gain, rim_pass, carry_pass):
    inner, gate, state_in, steps = projected
    tap_count = inner_kernel.shape[0]
    inner_width = inner.shape[-1]
    edge_rows = jnp.concatenate(
        [
            inner[:, inner.shape[1] - (tap_count - 1) :],
            state_in[:, state_in.shape[1] - (tap_count - 1) :],
        ],
        axis=-1,
    )
    rim_rows = rim_pass(edge_rows)
    inner_conv = convolve(inner, rim_rows[..., :inner_width], inner_kernel)
    state_conv = convolve(state_in, rim_rows[..., inner_width:], state_kernel)
    run_blocks = jax.vmap(
        partial(ssd_blocks, decay_rates=decay_rates, skip_gain=skip_gain, block_rows=BLOCK)
    )
    local_out, final_state = run_blocks(inner_conv, state_conv, steps)
    log_steps = -steps * decay_rates
    log_total = jnp.sum(log_steps, axis=1)
    log_cumul = jnp.cumsum(log_steps, axis=1)
    identity = (jnp.zeros_like(log_total), jnp.zeros_like(final_state))
    incoming = carry_pass((log_total, final_state), identity)
    state_count = state_conv.shape[-1] // 2
    read_rows = state_conv[..., state_count:].astype(jnp.float32)
    extra = jnp.exp(log_cumul)[..., None] * jnp.einsum(
        "wrn,whpn->wrhp", read_rows, incoming[1], precision=lax.Precision.HIGHEST
    )
    outputs = local_out + extra.reshape(local_out.shape)
    return outputs * jax.nn.silu(gate.astype(jnp.float32))


def forward_rim(edge_rows):
    return shifted(edge_rows, "seq", 1)


def forward_carry(pieces, identity):
    return prefix(pieces, "seq", combine_carry, identity)


def on_device(
    tokens,
    embedding,
    inner_weight,
    gate_weight,
    state_weight,
    step_weight,
    inner_kernel,
    state_kernel,
    step_bias,
    decay_rates,
    skip_gain,
    norm_gain,
    out_weight,
):
    front_proj = project(
        tokens, embedding, inner_weight, gate_weight, state_weight, step_weight, step_bias
    )
    complement = jnp.where(tokens < 4, 3 - tokens, 4)
    for bit_index in range(lax.axis_size("seq").bit_length() - 1):
        complement = from_partner(complement, "seq", bit_index)
    complement = complement[:, ::-1]
    back_proj = project(
        complement, embedding, inner_weight, gate_weight, state_weight, step_weight, step_bias
    )
    gated_front = mixer(
        front_proj, inner_kernel, state_kernel, decay_rates, skip_gain, forward_rim, forward_carry
    )
    gated_back = mixer(
        back_proj, inner_kernel, state_kernel, decay_rates, skip_gain, forward_rim, forward_carry
    )
    squares = lax.psum(
        (jnp.sum(gated_front * gated_front, axis=-1), jnp.sum(gated_back * gated_back, axis=-1)),
        "ch",
    )
    front_scale = lax.rsqrt(squares[0] / E + 1e-05)
    back_scale = lax.rsqrt(squares[1] / E + 1e-05)
    normed_front = (gated_front * front_scale[..., None] * norm_gain).astype(jnp.bfloat16)
    normed_back = (gated_back * back_scale[..., None] * norm_gain).astype(jnp.bfloat16)
    normed_back = normed_back[:, ::-1]
    for bit_index in range(lax.axis_size("seq").bit_length() - 1):
        normed_back = from_partner(normed_back, "seq", bit_index)
    front_term = jnp.einsum(
        "wre,ed->rwd", normed_front, out_weight, preferred_element_type=jnp.float32
    )
    back_term = jnp.einsum(
        "wre,ed->rwd", normed_back, out_weight, preferred_element_type=jnp.float32
    )
    summed = lax.psum_scatter(front_term + back_term, "ch", scatter_dimension=0, tiled=True)
    return summed.astype(jnp.bfloat16)


def solution(mesh):
    placed = (
        P(None, "seq"),
        P(),
        P(None, "ch"),
        P(None, "ch"),
        P(),
        P(None, "ch"),
        P(None, "ch"),
        P(),
        P("ch"),
        P("ch"),
        P("ch"),
        P("ch"),
        P("ch", None),
    )
    return jax.shard_map(
        on_device,
        mesh=mesh,
        in_specs=placed,
        out_specs=P(("seq", "ch"), None, None),
        check_vma=False,
    )
```

profile of v0, /device:TPU:0, one launch (start us, length us, event | category | flops | bytes accessed | tf_op | source)
XLA Modules:
  0.0 814.2 jit_solution(5551571806552675490)
XLA Ops:
  24.0 3.9 maximum_convert_fusion
  43.6 4.2 reduce-window.28
  50.6 4.2 reduce-window.34
  62.0 22.6 %all-gather.4 = f32[16,2,4]{2,1,0:T(2,128)} all-gather(f32[1,2,4]{2,1,0:T(2,128)S(1)} %bitcast.356), channel_id=2, replica_groups=mesh['seq'=16,'ch'=2] {'seq'}, dimensions={0}, use_global_device_ids=true | all-gather | bytes 544 | tf_op jit(solution)/shard_map/all_gather | solution.py:20
  84.5 18.1 %all-gather.5 = f32[16,2,4]{2,1,0:T(2,128)} all-gather(f32[1,2,4]{2,1,0:T(2,128)S(1)} %bitcast.355), channel_id=4, replica_groups=mesh['seq'=16,'ch'=2] {'seq'}, dimensions={0}, use_global_device_ids=true | all-gather | bytes 544 | tf_op jit(solution)/shard_map/all_gather | solution.py:20
  104.6 10.8 %fusion.102 = (f32[2,2048,256]{2,1,0:T(8,128)}, f32[2,2048,256]{2,1,0:T(8,128)}) fusion(f32[2,2051,256]{2,1,0:T(8,128)S(1)} %maximum_convert_fusion.1, f32[256]{0:T(256)} %bitcast.359, f32[256]{0:T(256)} %bitcast.360, f32[256]{0:T(256)} %bitcast.358, f32[256]{0:T(256)} %bitcast.357, f32[2,2051,256]{2,1,0:T(8,128)} %maximum_convert_fusion), kind=kLoop, calls=%fused_computation.153 | loop fusion | flops 27262976 | bytes 41947136 | tf_op jit(solution)/shard_map/vmap()/transpose | solution.py:83
  115.4 5.4 copy.164
  120.8 6.1 copy.209
  133.6 121.1 %while.58 = (s32[]{:T(128)}, f32[2,4,64,16]{2,3,1,0:T(8,128)S(1)}, f32[8,2,256,4,64]{2,4,3,1,0:T(8,128)}, f32[8,2,256,4]{2,3,1,0:T(4,128)}, f32[4]{0:T(128)}, /*...) while((s32[]{:T(128)}, f32[2,4,64,16]{2,3,1,0:T(8,128)S(1)}, ...), condition=%wide.region_3.4_spmd.clone.clone, body=%wide.region_0.3_spmd.clone.clone.sunk | while | flops 481433632 | bytes 5828683 | solution.py:83
  254.8 8.4 %copy.195 = f32[2,8,256,4,64]{4,3,2,1,0:T(4,128)} copy(f32[2,8,256,4,64]{2,4,3,0,1:T(8,128)} %bitcast.328) | data formatting | bytes 8388608 | tf_op jit(solution)/shard_map/vmap()/reshape | solution.py:84
  263.1 8.8 %reshape.226 = f32[2,2048,256]{2,1,0:T(8,128)} reshape(f32[2,8,256,4,64]{4,3,2,1,0:T(4,128)} %copy.195) | data formatting | bytes 8388608 | tf_op jit(solution)/shard_map/vmap()/reshape | solution.py:84
  271.9 22.5 %all-gather.1 = f32[32,4,64,16]{2,3,1,0:T(8,128)S(1)} all-gather(f32[2,4,64,16]{2,3,1,0:T(8,128)S(1)} %get-tuple-element.306), channel_id=3, replica_groups=mesh['seq'=16,'ch'=2] {'seq'}, dimensions={0}, use_global_device_ids=true | all-gather | bytes 557056 | tf_op jit(solution)/shard_map/all_gather | solution.py:20
  294.4 12.3 %while.56 = (s32[]{:T(128)}, f32[2,4,64,16]{2,3,1,0:T(8,128)S(1)}, s32[]{:T(128)}, f32[16,2,4]{2,1,0:T(2,128)}, f32[16,2,4,64,16]{3,4,2,1,0:T(8,128)S(1)}, /*index=5*/s32[]{:T(128)}, s32[]{:T(128)}) while((s32[]{:T(128)}, f32[2,4,64,16]{2,3,1,0:T(8,128)S(1)}, s32[]{:T(128)}, f32[16,2,4]{2,1,0:T(2,128)}, ...), condition=%wide.region_8.9_spmd.clone, body=%wide.region_7.8_spmd.clone.sunk | while | flops 32772 | bytes 98513 | solution.py:30
  306.7 4.7 convolution_multiply_fusion.3
  311.4 5.4 copy.171
  316.8 5.4 copy.176
  322.2 6.2 copy.210
  332.3 121.3 %while.59 = (s32[]{:T(128)}, f32[2,4,64,16]{2,3,1,0:T(8,128)S(1)}, f32[8,2,256,4,64]{2,4,3,1,0:T(8,128)}, f32[8,2,256,4]{2,3,1,0:T(4,128)}, f32[4]{0:T(128)}, /*...) while((s32[]{:T(128)}, f32[2,4,64,16]{2,3,1,0:T(8,128)S(1)}, ...), condition=%wide.region_14.15_spmd.clone.clone, body=%wide.region_11.14_spmd.clone.clone.sunk | while | flops 481433632 | bytes 5828187 | solution.py:83
  453.6 8.4 %copy.197 = f32[2,8,256,4,64]{4,3,2,1,0:T(4,128)} copy(f32[2,8,256,4,64]{2,4,3,0,1:T(8,128)} %bitcast.329) | data formatting | bytes 8388608 | tf_op jit(solution)/shard_map/vmap()/reshape | solution.py:84
  461.9 8.6 %reshape.227 = f32[2,2048,256]{2,1,0:T(8,128)} reshape(f32[2,8,256,4,64]{4,3,2,1,0:T(4,128)} %copy.197) | data formatting | bytes 8388608 | tf_op jit(solution)/shard_map/vmap()/reshape | solution.py:84
  470.5 20.9 %all-gather.3 = f32[32,4,64,16]{2,3,1,0:T(8,128)S(1)} all-gather(f32[2,4,64,16]{2,3,1,0:T(8,128)S(1)} %get-tuple-element.309), channel_id=5, replica_groups=mesh['seq'=16,'ch'=2] {'seq'}, dimensions={0}, use_global_device_ids=true | all-gather | bytes 557056 | tf_op jit(solution)/shard_map/all_gather | solution.py:20
  491.4 12.4 %while.57 = (s32[]{:T(128)}, f32[2,4,64,16]{2,3,1,0:T(8,128)S(1)}, s32[]{:T(128)}, f32[16,2,4]{2,1,0:T(2,128)}, f32[16,2,4,64,16]{3,4,2,1,0:T(8,128)S(1)}, /*index=5*/s32[]{:T(128)}, s32[]{:T(128)}) while((s32[]{:T(128)}, f32[2,4,64,16]{2,3,1,0:T(8,128)S(1)}, s32[]{:T(128)}, f32[16,2,4]{2,1,0:T(2,128)}, ...), condition=%wide.region_19.20_spmd.clone, body=%wide.region_18.19_spmd.clone.sunk | while | flops 32772 | bytes 98513 | solution.py:30
  503.8 4.7 convolution_multiply_fusion.2
  508.5 5.4 copy.183
  513.9 7.0 multiply_reduce_fusion.1
  524.8 8.3 %all-reduce = (f32[2,2048]{1,0:T(2,128)S(1)}, f32[2,2048]{1,0:T(2,128)S(1)}) all-reduce(f32[2,2048]{1,0:T(2,128)S(1)} %get-tuple-element.623, f32[2,2048]{1,0:T(2,128)S(1)} %get-tuple-element.625), channel_id=1, replica_groups=mesh['seq'=16,'ch'=2] {'ch'}, use_global_device_ids=true, to_apply=%region_10.11 | all-reduce | flops 8192 | bytes 65536 | tf_op jit(solution)/shard_map/psum | solution.py:198
  535.9 20.2 %rev.7 = bf16[2,2048,256]{2,1,0:T(8,128)(2,1)} reverse(bf16[2,2048,256]{2,1,0:T(8,128)(2,1)S(1)} %multiply_convert_fusion), dimensions={1} | reverse | bytes 4194304 | tf_op jit(solution)/shard_map/rev | solution.py:206
  556.1 4.4 collective-permute-done.6
  563.3 45.9 %collective-permute-done.7 = bf16[2,2048,256]{2,1,0:T(8,128)(2,1)S(1)} collective-permute-done((bf16[2,2048,256]{2,1,0:T(8,128)(2,1)S(1)}, bf16[2,2048,256]{2,1,0:T(8,128)(2,1)S(1)}, u32[]{:S(2)}, u32[]{:S(2)}) %collective-permute-start.7) | collective-permute-done | bytes 2097184 | tf_op jit(solution)/shard_map/ppermute | solution.py:36
  609.3 47.2 %collective-permute-done.8 = bf16[2,2048,256]{2,1,0:T(8,128)(2,1)S(1)} collective-permute-done((bf16[2,2048,256]{2,1,0:T(8,128)(2,1)S(1)}, bf16[2,2048,256]{2,1,0:T(8,128)(2,1)S(1)}, u32[]{:S(2)}, u32[]{:S(2)}) %collective-permute-start.8) | collective-permute-done | bytes 2097184 | tf_op jit(solution)/shard_map/ppermute | solution.py:36
  659.2 89.3 %collective-permute-done.9 = bf16[2,2048,256]{2,1,0:T(8,128)(2,1)S(1)} collective-permute-done((bf16[2,2048,256]{2,1,0:T(8,128)(2,1)S(1)}, bf16[2,2048,256]{2,1,0:T(8,128)(2,1)S(1)}, u32[]{:S(2)}, u32[]{:S(2)}) %collective-permute-start.9) | collective-permute-done | bytes 2097184 | tf_op jit(solution)/shard_map/ppermute | solution.py:36
  751.3 51.9 %reduce-scatter.2.cloned.1.call-done = f32[1024,2,256]{2,0,1:T(8,128)} async-done(((f32[2048,2,256]{2,0,1:T(8,128)}), f32[1024,2,256]{2,0,1:T(8,128)}) %reduce-scatter.2.cloned.1.call-update) | async-done | bytes 2097168 | tf_op jit(solution)/shard_map/reduce_scatter | solution.py:215
  (511 shorter events, 339.5 us)
Async XLA Ops:
  6.5 507.4 %copy-start = (bf16[256,256]{1,0:T(8,128)(2,1)S(1)}, bf16[256,256]{1,0:T(8,128)(2,1)}, u32[]{:S(2)}) copy-start(bf16[256,256]{1,0:T(8,128)(2,1)} %param.24) | copy-start | bytes 393220
  6.5 5.8 copy-start.11
  6.5 796.6 %reduce-scatter.2.cloned.1.call-start = ((), (), s32[]{:S(2)}) async-start(), calls=%async_computation.1 | async-start | bytes 6291456 | tf_op jit(solution)/shard_map/reduce_scatter | solution.py:215
  7.3 8.6 %copy-start.14 = (bf16[256,4]{0,1:T(4,128)(2,1)S(1)}, bf16[256,4]{0,1:T(4,128)(2,1)}, u32[]{:S(2)}) copy-start(bf16[256,4]{0,1:T(4,128)(2,1)} %param.26) | copy-start | bytes 6148
  7.3 8.6 %copy-start.22 = (f32[4]{0:T(128)S(1)}, f32[4]{0:T(128)}, u32[]{:S(2)}) copy-start(f32[4]{0:T(128)} %param.29) | copy-start | bytes 52
  7.3 9.9 %collective-permute-start.1 = (s32[2,2048]{1,0:T(2,128)S(1)}, s32[2,2048]{1,0:T(2,128)S(1)}, u32[]{:S(2)}, u32[]{:S(2)}) collective-permute-start(s32[2,2048]{1,0:T(2,128)S(1)} %compare_select_fusion.2), channel_id=1, source_target_pairs={{0,2},{2,0},{4,6},{6,4},{8,10},{10,8},{12,14},{14,12},{16,18},{18,... | collective-permute-start | bytes 49160 | tf_op jit(solution)/shard_map/ppermute | solution.py:36
  9.4 7.3 copy-start.15
  9.4 10.8 %copy-start.21 = (f32[4,32]{1,0:T(4,128)S(1)}, f32[4,32]{1,0:T(4,128)}, u32[]{:S(2)}) copy-start(f32[4,32]{1,0:T(4,128)} %param.28) | copy-start | bytes 1540
  14.0 20.2 %copy-start.13 = (bf16[5,256]{1,0:T(8,128)(2,1)S(1)}, bf16[5,256]{1,0:T(8,128)(2,1)}, u32[]{:S(2)}) copy-start(bf16[5,256]{1,0:T(8,128)(2,1)} %param.22) | copy-start | bytes 7684
  14.0 6.8 collective-permute-start
  17.2 4.7 collective-permute-start.2
  21.9 6.2 collective-permute-start.3
  28.1 4.7 collective-permute-start.4
  35.0 4.4 copy-start.1
  40.2 62.3 %collective-permute-start.5 = (bf16[2,3,288]{2,1,0:T(4,128)(2,1)S(1)}, bf16[2,3,288]{2,1,0:T(4,128)(2,1)S(1)}, u32[]{:S(2)}, u32[]{:S(2)}) collective-permute-start(bf16[2,3,288]{2,1,0:T(4,128)(2,1)S(1)} %pad_maximum_fusion.1), channel_id=1, source_target_pairs={{0,2},{2,4},{4,6},{6,8},{8,10},{10,12},{12,14},{14,16},{16,18},{18... | collective-permute-start | bytes 10376 | tf_op jit(solution)/shard_map/ppermute | solution.py:15
  120.8 6.3 copy-start.17
  120.8 6.4 copy-start.18
  120.8 6.4 copy-start.19
  120.8 6.4 copy-start.20
  128.1 5.5 copy-start.5
  322.2 6.2 copy-start.8
  322.2 6.9 copy-start.7
  461.9 41.9 %copy-start.10 = (f32[2,4,2048]{2,1,0:T(4,128)S(1)}, f32[2,4,2048]{2,1,0:T(4,128)}, u32[]{:S(2)}) copy-start(f32[2,4,2048]{2,1,0:T(4,128)} %exp.124) | copy-start | bytes 196612
  513.9 7.0 copy-start.2
  513.9 7.0 copy-start.3
  513.9 7.5 copy-start.4
  521.5 11.7 %copy-start.16 = (f32[256]{0:T(256)S(1)}, f32[256]{0:T(256)}, u32[]{:S(2)}) copy-start(f32[256]{0:T(256)} %param.32) | copy-start | bytes 3076
  533.2 123.2 %copy-start.9 = (bf16[256,256]{1,0:T(8,128)(2,1)S(1)}, bf16[256,256]{1,0:T(8,128)(2,1)}, u32[]{:S(2)}) copy-start(bf16[256,256]{1,0:T(8,128)(2,1)} %param.33) | copy-start | bytes 393220
  556.1 4.4 collective-permute-start.6
  560.5 48.8 %collective-permute-start.7 = (bf16[2,2048,256]{2,1,0:T(8,128)(2,1)S(1)}, bf16[2,2048,256]{2,1,0:T(8,128)(2,1)S(1)}, u32[]{:S(2)}, u32[]{:S(2)}) collective-permute-start(bf16[2,2048,256]{2,1,0:T(8,128)(2,1)S(1)} %collective-permute-done.6), channel_id=1, source_target_pairs={{0,4},{2,6},{4,0},{6,2},{8,12},{10,14},{12,8},{14,10},{16,20},{18,... | collective-permute-start | bytes 6291464 | tf_op jit(solution)/shard_map/ppermute | solution.py:36
  609.3 47.2 %collective-permute-start.8 = (bf16[2,2048,256]{2,1,0:T(8,128)(2,1)S(1)}, bf16[2,2048,256]{2,1,0:T(8,128)(2,1)S(1)}, u32[]{:S(2)}, u32[]{:S(2)}) collective-permute-start(bf16[2,2048,256]{2,1,0:T(8,128)(2,1)S(1)} %collective-permute-done.7), channel_id=1, source_target_pairs={{0,8},{2,10},{4,12},{6,14},{8,0},{10,2},{12,4},{14,6},{16,24},{18,... | collective-permute-start | bytes 6291464 | tf_op jit(solution)/shard_map/ppermute | solution.py:36
  656.4 92.1 %collective-permute-start.9 = (bf16[2,2048,256]{2,1,0:T(8,128)(2,1)S(1)}, bf16[2,2048,256]{2,1,0:T(8,128)(2,1)S(1)}, u32[]{:S(2)}, u32[]{:S(2)}) collective-permute-start(bf16[2,2048,256]{2,1,0:T(8,128)(2,1)S(1)} %collective-permute-done.8), channel_id=1, source_target_pairs={{0,16},{2,18},{4,20},{6,22},{8,24},{10,26},{12,28},{14,30},{16,0},... | collective-permute-start | bytes 6291464 | tf_op jit(solution)/shard_map/ppermute | solution.py:36
  (2 other events, 4.6 us)
Sparse Core Ops, SparseCore 0:
  751.4 51.7 reduce-scatter.1
where the time goes:
time: 826 us; the launch traced here: 814 us
  waiting for transfers between devices  242 us (29%)
  local copies, waits for them, and re-layouts  194 us (23%)
  matrix products  161 us (19%)
  other arithmetic  94.4 us (11%)
  blocking collectives  92.4 us (11%)
  starting transfers between devices  14.3 us (2%)
  between operations  14.2 us (2%)
    ppermute x8, waiting for transfers between devices, from_partner(): return lax.ppermute(value, axis, pairs)  190 us
    all_gather x4, blocking collectives, prefix(): everything = jax.tree.map(lambda part: lax.all_gather(part, axis), x)  84 us
    another operation x76, other arithmetic  56.5 us
    dot_general x16, matrix products, advance(): jnp.einsum('tsh,shp->thp', kernel, driven, precision=lax.Precision.HIGHEST)  52.8 us
    reduce_scatter x1, waiting for transfers between devices, on_device(): lax.psum_scatter(front_term + back_term, 'ch', scatter_dimension=0, tiled...  51.9 us
    dynamic_slice x16, local copies, waits for them, and re-layouts, ssd_blocks(): lax.scan(advance, zero_state, (input_all, key_all, read_all, step_all))  41.3 us
    dot_general x16, matrix products, advance(): jnp.einsum('tn,hpn->thp', read_rows, carry_state, precision=lax.Precision...  40.8 us
    reshape x4, local copies, waits for them, and re-layouts, ssd_blocks(): return (outputs.reshape(length, head_count * head_width), final_state)  34.1 us
  transfers between devices with their start and end apart: 11, of which 7 were waited for; matrix products, arithmetic and copies ran while one was open for 4% of the time, Pallas kernels for 0%

commit v1 on v0

v1 whole, which is shorter than its diff:
```python
from functools import partial

import jax
import jax.numpy as jnp
import numpy as np
from jax import lax
from jax.experimental import pallas as pl
from jax.experimental.pallas import tpu as pltpu
from jax.sharding import PartitionSpec as P

SUB = 64
ROWS = 256
EPS = 1e-05
COLS = 128


def split3(v):
    hi = lax.reduce_precision(v, 8, 7)
    rest = v - hi
    mid = lax.reduce_precision(rest, 8, 7)
    low = lax.reduce_precision(rest - mid, 8, 7)
    return hi, mid, low


def pieces(table):
    taps, ids, width = table.shape
    full = jnp.pad(table, ((0, 4 - taps), (0, 8 - ids), (0, 0))).reshape(32, width)
    stacked = jnp.concatenate(split3(full) + (jnp.zeros_like(full),), axis=0)
    return stacked.astype(jnp.bfloat16)


def silu(v):
    return v * (1.0 / (1.0 + jnp.exp(-v)))


def dot(a, b):
    return jnp.dot(a, b, preferred_element_type=jnp.float32)


def state_kernel_body(oh_ref, tri_ref, tx_ref, tst_ref, tdt_ref, ld_ref, x_ref, kv_ref, sloc_ref, sfin_ref):
    @pl.when(pl.program_id(1) == 0)
    def _():
        sfin_ref[...] = jnp.zeros_like(sfin_ref)

    oh = oh_ref[0]
    x = silu(dot(oh, tx_ref[...])).astype(jnp.bfloat16)
    x_ref[0] = x
    kv = silu(dot(oh, tst_ref[...])).astype(jnp.bfloat16)
    kv_ref[0] = kv
    cum = dot(dot(tri_ref[...], oh).astype(jnp.bfloat16), ld_ref[...])
    dt = dot(oh, tdt_ref[...])
    state = sfin_ref[0]
    for j in range(ROWS // SUB):
        rows = slice(j * SUB, (j + 1) * SUB)
        cum_j = cum[rows]
        tot = cum_j[SUB - 1 :]
        wx = (x[rows].astype(jnp.float32) * dt[rows] * jnp.exp(tot - cum_j)).astype(jnp.bfloat16)
        new = lax.dot_general(
            kv[rows, :16], wx, (((0,), (0,)), ((), ())), preferred_element_type=jnp.float32
        )
        sloc_ref[0, j] = new
        state = jnp.exp(tot) * state + new
    sfin_ref[0] = state


def output_kernel_body(
    oh_ref, x_ref, kv_ref, sloc_ref, inc_ref, tri_ref, tdt_ref, tsg_ref, ld_ref,
    skip_ref, gain_ref, ow_ref, causal_ref, diag_ref, bd_ref, flip_ref,
    out_ref, state_ref, front_ref,
):
    strand, sb = pl.program_id(1), pl.program_id(2)
    count = pl.num_programs(2)

    @pl.when(sb == 0)
    def _():
        state_ref[...] = inc_ref[0]

    oh = oh_ref[0]
    cum = dot(dot(tri_ref[...], oh).astype(jnp.bfloat16), ld_ref[...])
    dt = dot(oh, tdt_ref[...])
    sg = dot(oh, tsg_ref[...])
    skip, gain = skip_ref[...], gain_ref[...]
    causal, diag, bd = causal_ref[...], diag_ref[...], bd_ref[...]
    state = state_ref[...]
    parts = []
    for j in range(ROWS // SUB):
        rows = slice(j * SUB, (j + 1) * SUB)
        cum_j = cum[rows]
        tot = cum_j[SUB - 1 :]
        xj = x_ref[0, rows, :].astype(jnp.float32)
        driven = (xj * dt[rows]).astype(jnp.bfloat16)
        key, read = kv_ref[0, rows, :16], kv_ref[0, rows, 16:32]
        crow = jnp.sum(cum_j * diag, axis=0, keepdims=True)
        rk = lax.dot_general(
            read, jnp.concatenate([key, key], axis=0), (((1,), (1,)), ((), ())),
            preferred_element_type=jnp.float32,
        )
        rk = jnp.concatenate([rk] * 4, axis=1)
        kmat = (jnp.exp(jnp.minimum(cum_j - crow, 0.0)) * causal * rk).astype(jnp.bfloat16)
        within = []
        for g in range(2):
            lanes = slice(g * 256, (g + 1) * 256)
            rhs = jnp.concatenate([driven[:, lanes]] * 4, axis=0) * bd
            within.append(dot(kmat[:, lanes], rhs))
        carried = jnp.exp(cum_j) * dot(read, state.astype(jnp.bfloat16))
        y = jnp.concatenate(within, axis=1) + carried + skip * xj
        state = jnp.exp(tot) * state + sloc_ref[0, j]
        gated = y * sg[rows]
        mean = jnp.mean(gated * gated, axis=-1, keepdims=True)
        parts.append((gated * lax.rsqrt(mean + EPS) * gain).astype(jnp.bfloat16))
    state_ref[...] = state
    normed = jnp.concatenate(parts, axis=0)

    @pl.when(strand == 0)
    def _():
        front_ref[pl.ds(pl.multiple_of(sb * ROWS, ROWS), ROWS), :] = normed

    @pl.when(strand == 1)
    def _():
        back = dot(flip_ref[...], normed).astype(jnp.bfloat16)
        start = pl.multiple_of((count - 1 - sb) * ROWS, ROWS)
        front = front_ref[pl.ds(start, ROWS), :]
        ow = ow_ref[...]
        out_ref[...] = (dot(front, ow) + dot(back, ow)).astype(out_ref.dtype)


def whole_spec(array):
    return pl.BlockSpec(array.shape, lambda *_: (0,) * array.ndim)


def on_device(
    tokens, embedding, inner_weight, gate_weight, state_weight, step_weight, inner_kernel,
    state_kernel, step_bias, decay_rates, skip_gain, norm_gain, out_weight,
):
    f32, bf16 = jnp.float32, jnp.bfloat16
    wins, held = tokens.shape
    chs, seqs = lax.axis_size("ch"), lax.axis_size("seq")
    ch, seq = lax.axis_index("ch"), lax.axis_index("seq")
    rows = held // chs
    devices = seqs * chs
    me = seq * chs + ch
    heads_here = decay_rates.shape[0]
    width = inner_weight.shape[1]
    head_width = width // heads_here

    inner_tab = dot(embedding, inner_weight).astype(bf16).astype(f32)
    gate_tab = dot(embedding, gate_weight).astype(bf16).astype(f32)
    state_tab = dot(embedding, state_weight).astype(bf16).astype(f32)
    step_tab = jax.nn.softplus(dot(embedding, step_weight) + step_bias)
    spread = lambda v: jnp.repeat(v, head_width, axis=-1)
    packed = jnp.concatenate(
        [
            inner_tab,
            jax.nn.silu(gate_tab),
            spread(step_tab),
            spread(-step_tab * decay_rates),
            inner_kernel,
            spread(skip_gain)[None],
            norm_gain[None],
        ],
        axis=0,
    )
    packed = lax.all_gather(packed, "ch", axis=1, tiled=True)
    ow = lax.all_gather(out_weight, "ch", axis=0, tiled=True)
    inner_all, sg_all, step_all, ld_all = (packed[5 * i : 5 * i + 5] for i in range(4))
    taps_all, skip_all, gain_all = packed[20:24], packed[24:25], packed[25:26]
    tx = pieces(taps_all[:, None, :] * inner_all[None])
    tst = pieces(jnp.pad(state_kernel[:, None, :] * state_tab[None], ((0, 0), (0, 0), (0, 96))))
    tdt, tsg, ld = pieces(step_all[None]), pieces(sg_all[None]), pieces(ld_all[None])

    halves = tokens.reshape(wins, chs, rows)
    base = jnp.arange(5, dtype=jnp.int32)
    counts = jnp.sum((halves[..., None] == base).astype(jnp.int32), axis=2)
    info = jnp.concatenate(
        [counts.reshape(wins, chs * 5), tokens[:, :3], tokens[:, held - 3 :]], axis=1
    )
    info = lax.all_gather(info, "seq")
    none = 7
    edge = info[:, :, chs * 5 :]
    before = jnp.where(seq > 0, edge[jnp.maximum(seq - 1, 0)][:, 3:], none)
    after = jnp.where(seq < seqs - 1, edge[jnp.minimum(seq + 1, seqs - 1)][:, :3], none)
    around = jnp.concatenate([before, tokens, after], axis=1)
    mine = lax.dynamic_slice_in_dim(around, ch * rows, rows + 6, axis=1)
    other = jnp.where(mine < 4, 3 - mine, mine)[:, ::-1]
    ids = jnp.stack([mine, other], axis=1).reshape(wins * 2, rows + 6)
    column = np.arange(COLS)
    tap_of, id_of = (column // 8) % 4, column % 8
    onehot = jnp.zeros((wins * 2, rows, COLS), jnp.bool_)
    for k in range(4):
        tap = ids[:, 3 - k : 3 - k + rows, None] == jnp.asarray(id_of, jnp.int32)
        onehot = onehot | (tap & jnp.asarray(tap_of == k))
    onehot = onehot.astype(bf16)

    streams, steps = wins * 2, rows // ROWS
    subs = ROWS // SUB
    full = width * chs
    index = np.arange(ROWS)
    tri = jnp.asarray(
        (index[:, None] >= index[None]) & (index[:, None] // SUB == index[None] // SUB), bf16
    )
    row_spec = lambda n: pl.BlockSpec((1, ROWS, n), lambda s, b: (s, b, 0))
    x, kv, sloc, sfin = pl.pallas_call(
        state_kernel_body,
        grid=(streams, steps),
        in_specs=[row_spec(COLS)] + [whole_spec(v) for v in (tri, tx, tst, tdt, ld)],
        out_specs=[
            row_spec(full),
            row_spec(128),
            pl.BlockSpec((1, subs, 16, full), lambda s, b: (s, b, 0, 0)),
            pl.BlockSpec((1, 16, full), lambda s, b: (s, 0, 0)),
        ],
        out_shape=[
            jax.ShapeDtypeStruct((streams, rows, full), bf16),
            jax.ShapeDtypeStruct((streams, rows, 128), bf16),
            jax.ShapeDtypeStruct((streams, steps * subs, 16, full), f32),
            jax.ShapeDtypeStruct((streams, 16, full), f32),
        ],
        compiler_params=pltpu.CompilerParams(vmem_limit_bytes=40 << 20),
        name="states",
    )(onehot, tri, tx, tst, tdt, ld)

    gathered = lax.all_gather(sfin.astype(bf16), ("seq", "ch"))
    every = info[:, :, : chs * 5].reshape(seqs, wins, chs, 5)
    every = jnp.moveaxis(every, 2, 1).reshape(devices, wins, 5).astype(f32)
    j, m = np.arange(devices)[:, None], np.arange(devices)[None]
    fwd = (j < m) & (m < me)
    bwd = (j > m) & (m > me)
    between = jnp.stack(
        [
            jnp.sum(jnp.where(fwd[..., None, None], every[None], 0.0), axis=1),
            jnp.sum(jnp.where(bwd[..., None, None], every[None][..., jnp.array([3, 2, 1, 0, 4])], 0.0), axis=1),
        ],
        axis=2,
    )
    log_weight = jnp.sum(between[..., None] * ld_all, axis=3)
    who = np.arange(devices)
    reached = jnp.stack([who < me, who > me], axis=1)[:, None, :, None]
    weight = jnp.where(reached, jnp.exp(log_weight), 0.0).reshape(devices, streams, 1, full)
    incoming = jnp.sum(weight * gathered.astype(f32), axis=0)

    lane, t = np.arange(full)[None], np.arange(SUB)[:, None]
    causal = jnp.asarray(t >= lane % SUB, f32)
    diag = jnp.asarray(t == lane % SUB, f32)
    bd = jnp.asarray(np.arange(256)[:, None] // 64 == np.arange(256)[None] // 64, bf16)
    flip = jnp.asarray(np.eye(ROWS)[::-1], bf16)
    stream = lambda shape: pl.BlockSpec(
        (1,) + shape, lambda w, s, b: (w * 2 + s, b) + (0,) * (len(shape) - 1)
    )
    consts = (tri, tdt, tsg, ld, skip_all, gain_all, ow, causal, diag, bd, flip)
    model = out_weight.shape[1]
    out = pl.pallas_call(
        output_kernel_body,
        grid=(wins, 2, steps),
        in_specs=[
            stream((ROWS, COLS)),
            stream((ROWS, full)),
            stream((ROWS, 128)),
            stream((subs, 16, full)),
            pl.BlockSpec((1, 16, full), lambda w, s, b: (w * 2 + s, 0, 0)),
        ]
        + [whole_spec(v) for v in consts],
        out_specs=pl.BlockSpec((ROWS, model), lambda w, s, b: (steps - 1 - b * s, w)),
        out_shape=jax.ShapeDtypeStruct((rows, wins * model), bf16),
        scratch_shapes=[pltpu.VMEM((16, full), f32), pltpu.VMEM((rows, full), bf16)],
        compiler_params=pltpu.CompilerParams(vmem_limit_bytes=40 << 20),
        name="outputs",
    )(onehot, x, kv, sloc, incoming, *consts)
    return out.reshape(rows, wins, model)


def solution(mesh):
    placed = (
        P(None, "seq"), P(), P(None, "ch"), P(None, "ch"), P(), P(None, "ch"), P(None, "ch"), P(),
        P("ch"), P("ch"), P("ch"), P("ch"), P("ch", None),
    )
    return jax.shard_map(
        on_device,
        mesh=mesh,
        in_specs=placed,
        out_specs=P(("seq", "ch"), None, None),
        check_vma=False,
    )
```

time: 826 us -> 164 us (0.20); the launches traced: 814 us -> 163 us
  waiting for transfers between devices: 242 us -> 45.3 us
  local copies, waits for them, and re-layouts: 194 us -> 21.7 us
  matrix products: 161 us -> 3.6 us
  other arithmetic: 94.4 us -> 8.29 us
  blocking collectives: 92.4 us -> 34.2 us
  Pallas kernels: 0 us -> 36 us
  starting transfers between devices: 14.3 us -> 0.04 us
    ppermute x10 -> x0, waiting for transfers between devices: 190 us -> none  [the longest x8 190 us: from_partner(): return lax.ppermute(value, axis, pairs)]
    dot_general x78 -> x4, matrix products: 161 us -> 3.6 us  [dot(): return jnp.dot(a, b, preferred_element_type=jnp.float32)]
    another operation x76 -> x8, other arithmetic: 56.5 us -> 0.17 us  [the longest x2 0.09 us: on_device(): ids = jnp.stack([mine, other], axis=1).reshape(wins * 2, rows + 6)]
    reduce_scatter x1 -> x0, waiting for transfers between devices: 51.9 us -> none  [on_device(): lax.psum_scatter(front_term + back_term, 'ch', scatter_dimension=0, tiled...]
    all_gather x4 -> x3, blocking collectives: 84 us -> 34.2 us  [the longest x1 22.2 us: on_device(): info = lax.all_gather(info, 'seq')]
    reshape x16 -> x5, local copies, waits for them, and re-layouts: 47.9 us -> 1.38 us  [the longest x1 1.11 us: on_device(): return out.reshape(rows, wins, model)]
    all_gather x0 -> x1, waiting for transfers between devices: none -> 45.3 us  [on_device(): gathered = lax.all_gather(sfin.astype(bf16), ('seq', 'ch'))]
    dynamic_slice x16 -> x0, local copies, waits for them, and re-layouts: 41.3 us -> none  [ssd_blocks(): lax.scan(advance, zero_state, (input_all, key_all, read_all, step_all))]
  transfers between devices with their start and end apart: 11 -> 1, of which waited for: 7 -> 1; matrix products, arithmetic and copies ran while one was open for 4% -> 1% of each run, Pallas kernels for 0% -> 0%
where the time goes in v1:
time: 164 us; the launch traced here: 163 us
  waiting for transfers between devices  45.3 us (28%)
  Pallas kernels  36 us (22%)
  blocking collectives  34.2 us (21%)
  local copies, waits for them, and re-layouts  21.7 us (13%)
  between operations  13.8 us (8%)
  other arithmetic  8.29 us (5%)
  matrix products  3.6 us (2%)
    all_gather x1, waiting for transfers between devices, on_device(): gathered = lax.all_gather(sfin.astype(bf16), ('seq', 'ch'))  45.3 us
    pallas_call x1, Pallas kernels, on_device(): pl.pallas_call(output_kernel_body, grid=(wins, 2, steps), in_specs=[strea...  25.6 us
    all_gather x1, blocking collectives, on_device(): info = lax.all_gather(info, 'seq')  22.2 us
    unnamed x47, local copies, waits for them, and re-layouts  13.4 us
    pallas_call x1, Pallas kernels, on_device(): pl.pallas_call(state_kernel_body, grid=(streams, steps), in_specs=[row_sp...  10.4 us
    all_gather x1, blocking collectives, on_device(): ow = lax.all_gather(out_weight, 'ch', axis=0, tiled=True)  6.49 us
    all_gather x1, blocking collectives, on_device(): packed = lax.all_gather(packed, 'ch', axis=1, tiled=True)  5.47 us
    dot_general x4, matrix products, dot(): return jnp.dot(a, b, preferred_element_type=jnp.float32)  3.6 us
  transfers between devices with their start and end apart: 1, of which 1 were waited for; matrix products, arithmetic and copies ran while one was open for 1% of the time, Pallas kernels for 0%

profile of v1, /device:TPU:0, one launch (start us, length us, event | category | flops | bytes accessed | tf_op | source)
XLA Modules:
  0.0 162.9 jit_solution(14405448511183197083)
XLA Ops:
  6.6 0.8 fusion.18
  7.4 0.8 eq.32
  8.2 0.8 fusion.2
  9.1 1.1 divide_multiply_fusion
  10.1 0.8 negate_multiply_fusion
  11.5 0.7 broadcast_in_dim.110
  12.3 1.5 concatenate.34
  13.9 5.5 %all_gather.20 = f32[26,512]{1,0:T(8,128)S(1)} all-gather(f32[26,256]{1,0:T(8,128)S(1)} %concatenate.34), channel_id=1, replica_groups=mesh['seq'=16,'ch'=2] {'ch'}, dimensions={1}, use_global_device_ids=true | all-gather | bytes 79872 | tf_op jit(solution)/shard_map/all_gather | solution.py:163
  19.9 22.2 %all-gather.2 = s32[16,2,16]{2,1,0:T(2,128)S(1)} all-gather(s32[1,2,16]{2,1,0:T(2,128)S(1)} %add_bitcast_fusion), channel_id=2, replica_groups=mesh['seq'=16,'ch'=2] {'seq'}, dimensions={0}, use_global_device_ids=true | all-gather | bytes 2176 | tf_op jit(solution)/shard_map/all_gather | solution.py:177
  42.2 0.8 concatenate.33
  43.2 0.8 reverse
  44.2 0.9 fusion.3
  45.1 0.7 broadcast_multiply_fusion.1
  46.1 2.8 %or_convert_fusion.oh_ref = bf16[4,1024,128]{2,1,0:T(8,128)(2,1)S(1)} fusion(s32[4,1024]{1,0:T(4,128)S(1)} %get-tuple-element.24, s32[4,1024]{1,0:T(4,128)S(1)} %get-tuple-element.25, s32[4,1024]{1,0:T(4,128)S(1)} %get-tuple-element.26, s32[128]{0:T(128)S(1)} %copy-done.16, s32[4,1024]{1,0:T(4,128)S(1)} %get-tuple-element.23, ...), kind=kLoop, calls=%fused_computation.3 | loop fusion | flops 6291456 | bytes 1115136 | tf_op jit(solution)/shard_map/convert_element_type | solution.py:192
  48.9 0.8 maximum_maximum_fusion.3
  49.7 10.4 %states.1 = (bf16[4,1024,512]{2,1,0:T(8,128)(2,1)S(1)}, bf16[4,1024,128]{2,1,0:T(8,128)(2,1)S(1)}, f32[4,16,16,512]{3,2,1,0:T(8,128)S(1)}, f32[4,16,512]{2,1,0:T(8,128)S(1)}) custom-call(bf16[4,1024,128]{2,1,0:T(8,128)(2,1)S(1)} %or_convert_fusion.oh_ref, bf16[256,256]{1,0:T(8,128)(2,1)S(1)} %copy-done.6, bf16[128,512]{1,0:T(8,128)(2,1)S(1)} %get-tuple-element.50.tx_ref, ...), custom_call_target="tpu_custom_call" | custom-call | tf_op jit(solution)/shard_map/states/pallas_call | solution.py:202
  60.1 1.9 %copy-done.1 = bf16[4,1024,512]{2,1,0:T(8,128)(2,1)} copy-done((bf16[4,1024,512]{2,1,0:T(8,128)(2,1)}, bf16[4,1024,512]{2,1,0:T(8,128)(2,1)S(1)}, u32[]{:S(2)}) %copy-start.1) | copy-done | bytes 4194328
  62.1 1.3 copy-done.3
  63.4 0.6 convert_element_type.73
  66.2 6.5 %all_gather.23.ow_ref = bf16[512,256]{1,0:T(8,128)(2,1)} all-gather(bf16[256,256]{1,0:T(8,128)(2,1)S(1)} %copy-done.13), channel_id=1, replica_groups=mesh['seq'=16,'ch'=2] {'ch'}, dimensions={0}, use_global_device_ids=true | all-gather | bytes 393216 | tf_op jit(solution)/shard_map/all_gather | solution.py:164
  72.7 45.3 %all-gather.5.cloned.1.call-done = bf16[128,16,512]{2,1,0:T(8,128)(2,1)} async-done(((bf16[4,16,512]{2,1,0:T(8,128)(2,1)}), bf16[128,16,512]{2,1,0:T(8,128)(2,1)}) %all-gather.5.cloned.1.call-update) | async-done | bytes 2097168 | tf_op jit(solution)/shard_map/all_gather | solution.py:222
  118.0 2.2 %fusion.inc_ref = f32[4,16,512]{2,1,0:T(8,128)S(1)} fusion(bf16[32,4,16,512]{3,2,1,0:T(8,128)(2,1)} %bitcast.86, f32[32,4,512]{2,1,0:T(4,128)S(1)} %copy.85), kind=kLoop, calls=%fused_computation.2 | loop fusion | flops 3112960 | bytes 2490368 | tf_op jit(solution)/shard_map/reduce_sum | solution.py:239
  120.2 2.2 %copy-done.2 = bf16[4,1024,512]{2,1,0:T(8,128)(2,1)S(1)} copy-done((bf16[4,1024,512]{2,1,0:T(8,128)(2,1)S(1)}, bf16[4,1024,512]{2,1,0:T(8,128)(2,1)}, u32[]{:S(2)}) %copy-start.2) | copy-done | bytes 4194328
  122.4 1.6 copy-done.4
  124.0 0.9 copy-done.7
  124.9 0.9 copy-done.8
  125.8 0.9 copy-done.9
  126.7 0.9 copy-done.10
  127.6 0.9 copy-done.11
  128.5 0.9 copy-done.12
  129.4 25.6 %outputs.1 = bf16[1024,512]{1,0:T(8,128)(2,1)S(1)} custom-call(bf16[4,1024,128]{2,1,0:T(8,128)(2,1)S(1)} %or_convert_fusion.oh_ref, bf16[4,1024,512]{2,1,0:T(8,128)(2,1)S(1)} %copy-done.2, bf16[4,1024,128]{2,1,0:T(8,128)(2,1)S(1)} %get-tuple-element.10.kv_ref, f32[4,16,16,512]{3,2,1,0:T(8,128)S(1)} %copy-done.4, f32[4,16,512]{2,1,0:T(8,128)S(1)} %fusion.inc_ref, ...), custom_call_target="tpu_custom_call" | custom-call | tf_op jit(solution)/shard_map/outputs/pallas_call | solution.py:251
  155.0 1.1 reshape.87
  (94 shorter events, 3.8 us)
Async XLA Ops:
  6.5 1.7 %copy-start = (bf16[256,256]{1,0:T(8,128)(2,1)S(1)}, bf16[256,256]{1,0:T(8,128)(2,1)}, u32[]{:S(2)}) copy-start(bf16[256,256]{1,0:T(8,128)(2,1)} %param.33) | copy-start | bytes 393220
  6.5 39.5 %copy-start.16 = (s32[128]{0:T(128)S(1)}, s32[128]{0:T(128)}, u32[]{:S(2)}) copy-start(s32[128]{0:T(128)} %constant.76.clone) | copy-start | bytes 1540
  6.5 39.5 %copy-start.17 = (pred[128]{0:T(512)(128)(4,1)S(1)}, pred[128]{0:T(512)(128)(4,1)}, u32[]{:S(2)}) copy-start(pred[128]{0:T(512)(128)(4,1)} %constant.80.clone) | copy-start | bytes 388
  6.5 39.5 %copy-start.18 = (pred[128]{0:T(512)(128)(4,1)S(1)}, pred[128]{0:T(512)(128)(4,1)}, u32[]{:S(2)}) copy-start(pred[128]{0:T(512)(128)(4,1)} %constant.79.clone) | copy-start | bytes 388
  6.5 39.5 %copy-start.19 = (pred[128]{0:T(512)(128)(4,1)S(1)}, pred[128]{0:T(512)(128)(4,1)}, u32[]{:S(2)}) copy-start(pred[128]{0:T(512)(128)(4,1)} %constant.78.clone) | copy-start | bytes 388
  6.6 39.5 %copy-start.20 = (pred[128]{0:T(512)(128)(4,1)S(1)}, pred[128]{0:T(512)(128)(4,1)}, u32[]{:S(2)}) copy-start(pred[128]{0:T(512)(128)(4,1)} %constant.77.clone) | copy-start | bytes 388
  6.6 111.4 %all-gather.5.cloned.1.call-start = ((), (), s32[]{:S(2)}) async-start(), calls=%async_computation | async-start | bytes 2162688 | tf_op jit(solution)/shard_map/all_gather | solution.py:222
  7.4 42.3 %copy-start.6 = (bf16[256,256]{1,0:T(8,128)(2,1)S(1)}, bf16[256,256]{1,0:T(8,128)(2,1)}, u32[]{:S(2)}) copy-start(bf16[256,256]{1,0:T(8,128)(2,1)} %constant.81.clone.tri_ref) | copy-start | bytes 393220
  46.0 18.6 %copy-start.21 = (s32[5]{0:T(128)S(1)}, s32[5]{0:T(128)}, u32[]{:S(2)}) copy-start(s32[5]{0:T(128)} %constant.106) | copy-start | bytes 64
  46.1 19.2 %copy-start.22 = (s32[1,32]{1,0:T(1,128)S(1)}, s32[1,32]{1,0:T(1,128)}, u32[]{:S(2)}) copy-start(s32[1,32]{1,0:T(1,128)} %constant.82.clone) | copy-start | bytes 388
  46.1 19.2 %copy-start.14 = (pred[32,32]{1,0:T(32,128)(4,1)S(1)}, pred[32,32]{1,0:T(32,128)(4,1)}, u32[]{:S(2)}) copy-start(pred[32,32]{1,0:T(32,128)(4,1)} %constant.84.clone) | copy-start | bytes 3076
  46.1 19.2 %copy-start.15 = (pred[32,32]{1,0:T(32,128)(4,1)S(1)}, pred[32,32]{1,0:T(32,128)(4,1)}, u32[]{:S(2)}) copy-start(pred[32,32]{1,0:T(32,128)(4,1)} %constant.83.clone) | copy-start | bytes 3076
  49.7 16.4 %copy-start.13 = (bf16[256,256]{1,0:T(8,128)(2,1)S(1)}, bf16[256,256]{1,0:T(8,128)(2,1)}, u32[]{:S(2)}) copy-start(bf16[256,256]{1,0:T(8,128)(2,1)} %param.43) | copy-start | bytes 393220
  60.1 1.9 %copy-start.1 = (bf16[4,1024,512]{2,1,0:T(8,128)(2,1)}, bf16[4,1024,512]{2,1,0:T(8,128)(2,1)S(1)}, u32[]{:S(2)}) copy-start(bf16[4,1024,512]{2,1,0:T(8,128)(2,1)S(1)} %get-tuple-element.9.x_ref) | copy-start | bytes 12582916
  62.1 1.4 copy-start.3
  118.0 2.2 %copy-start.5 = (bf16[512,256]{1,0:T(8,128)(2,1)S(1)}, bf16[512,256]{1,0:T(8,128)(2,1)}, u32[]{:S(2)}) copy-start(bf16[512,256]{1,0:T(8,128)(2,1)} %all_gather.23.ow_ref) | copy-start | bytes 786436
  120.2 2.2 %copy-start.2 = (bf16[4,1024,512]{2,1,0:T(8,128)(2,1)S(1)}, bf16[4,1024,512]{2,1,0:T(8,128)(2,1)}, u32[]{:S(2)}) copy-start(bf16[4,1024,512]{2,1,0:T(8,128)(2,1)} %copy-done.1) | copy-start | bytes 12582916
  122.4 1.6 copy-start.4
  124.0 0.9 copy-start.7
  124.9 0.9 copy-start.8
  125.8 0.9 copy-start.9
  126.7 0.9 copy-start.10
  127.6 0.9 copy-start.11
  128.5 0.9 copy-start.12
Sparse Core Ops, SparseCore 0:
  64.2 53.7 all-gather.4

commit v2 on v1

--- a/solution.py
+++ b/solution.py
@@ -37,10 +37,10 @@
     return jnp.dot(a, b, preferred_element_type=jnp.float32)
 
 
-def state_kernel_body(oh_ref, tri_ref, tx_ref, tst_ref, tdt_ref, ld_ref, x_ref, kv_ref, sloc_ref, sfin_ref):
+def state_kernel_body(oh_ref, tri_ref, tx_ref, tst_ref, tdt_ref, ld_ref, x_ref, kv_ref, sloc_ref, sfin_ref, state_ref):
     @pl.when(pl.program_id(1) == 0)
     def _():
-        sfin_ref[...] = jnp.zeros_like(sfin_ref)
+        state_ref[...] = jnp.zeros_like(state_ref)
 
     oh = oh_ref[0]
     x = silu(dot(oh, tx_ref[...])).astype(jnp.bfloat16)
@@ -49,7 +49,7 @@
     kv_ref[0] = kv
     cum = dot(dot(tri_ref[...], oh).astype(jnp.bfloat16), ld_ref[...])
     dt = dot(oh, tdt_ref[...])
-    state = sfin_ref[0]
+    state = state_ref[...]
     for j in range(ROWS // SUB):
         rows = slice(j * SUB, (j + 1) * SUB)
         cum_j = cum[rows]
@@ -60,7 +60,10 @@
         )
         sloc_ref[0, j] = new
         state = jnp.exp(tot) * state + new
-    sfin_ref[0] = state
+    state_ref[...] = state
+    half = state.shape[1] // 2
+    sfin_ref[0] = state[:, :half].astype(jnp.bfloat16)
+    sfin_ref[1] = state[:, half:].astype(jnp.bfloat16)
 
 
 def output_kernel_body(
@@ -73,7 +76,7 @@
 
     @pl.when(sb == 0)
     def _():
-        state_ref[...] = inc_ref[0]
+        state_ref[...] = jnp.concatenate([inc_ref[0], inc_ref[1]], axis=1).astype(jnp.float32)
 
     oh = oh_ref[0]
     cum = dot(dot(tri_ref[...], oh).astype(jnp.bfloat16), ld_ref[...])
@@ -124,6 +127,150 @@
         out_ref[...] = (dot(front, ow) + dot(back, ow)).astype(out_ref.dtype)
 
 
+MESH = pl.DeviceIdType.MESH
+GROUP = 8
+
+
+def exchange_body(
+    chs, devices, info_ref, packed_ref, ow_ref, info_out, packed_out, ow_out,
+    info_all, packed_all, ow_all, send, recv, psend, precv, osend, orecv,
+):
+    seq, ch = lax.axis_index("seq"), lax.axis_index("ch")
+    me = seq * chs + ch
+    place = lambda d: (d // chs, lax.rem(d, chs))
+    barrier = pltpu.get_barrier_semaphore()
+
+    def greet(d, _):
+        pl.semaphore_signal(
+            barrier, inc=1, device_id=place(lax.rem(me + d, devices)), device_id_type=MESH
+        )
+        return 0
+
+    lax.fori_loop(1, devices, greet, 0)
+    pl.semaphore_wait(barrier, devices - 1)
+
+    def remote(src, dst, ssem, rsem, device):
+        return pltpu.make_async_remote_copy(
+            src_ref=src, dst_ref=dst, send_sem=ssem, recv_sem=rsem, device_id=device,
+            device_id_type=MESH,
+        )
+
+    def info_copy(d, slot):
+        return remote(
+            info_ref, info_all.at[slot], send.at[d], recv.at[d], place(lax.rem(me + d, devices))
+        )
+
+    def start(d, _):
+        info_copy(d, me).start()
+        return 0
+
+    def finish(d, _):
+        info_copy(d, lax.rem(me + devices - d, devices)).wait()
+        return 0
+
+    def table_copies(d, slot):
+        device = (seq, lax.rem(ch + d, chs))
+        return (
+            remote(packed_ref, packed_all.at[slot], psend.at[d], precv.at[d], device),
+            remote(ow_ref, ow_all.at[slot], osend.at[d], orecv.at[d], device),
+        )
+
+    for d in range(1, chs):
+        for copy in table_copies(d, ch):
+            copy.start()
+    lax.fori_loop(1, devices, start, 0)
+    info_all[me] = info_ref[...]
+    packed_all[ch] = packed_ref[...]
+    ow_all[ch] = ow_ref[...]
+    for d in range(1, chs):
+        for copy in table_copies(d, lax.rem(ch + chs - d, chs)):
+            copy.wait()
+    lax.fori_loop(1, devices, finish, 0)
+    info_out[...] = info_all[...]
+    packed_out[...] = packed_all[...]
+    ow_out[...] = ow_all[...]
+
+
+def carry_body(
+    chs, groups, s_ref, log_ref, out_ref, first, total, second, third, landed,
+    send1, recv1, send2, recv2, send3, recv3,
+):
+    me = lax.axis_index("seq") * chs + lax.axis_index("ch")
+    g, q = me // GROUP, lax.rem(me, GROUP)
+    strand = lax.rem(q // 2, 2)
+    place = lambda d: (d // chs, lax.rem(d, chs))
+    mate = lambda d: place(g * GROUP + lax.rem(q + d, GROUP))
+    peer = lambda d: place(lax.rem(g + d, groups) * GROUP + q)
+    barrier = pltpu.get_barrier_semaphore()
+    for d in range(1, GROUP):
+        pl.semaphore_signal(barrier, inc=1, device_id=mate(d), device_id_type=MESH)
+
+    def greet(d, _):
+        pl.semaphore_signal(barrier, inc=1, device_id=peer(d), device_id_type=MESH)
+        return 0
+
+    lax.fori_loop(1, groups, greet, 0)
+    pl.semaphore_wait(barrier, GROUP - 1 + groups - 1)
+
+    def remote(src, dst, ssem, rsem, device):
+        return pltpu.make_async_remote_copy(
+            src_ref=src, dst_ref=dst, send_sem=ssem, recv_sem=rsem, device_id=device,
+            device_id_type=MESH,
+        )
+
+    def within(source, target, ssem, rsem, d, slot):
+        return remote(source.at[lax.rem(q + d, GROUP)], target.at[slot], ssem.at[d], rsem.at[d], mate(d))
+
+    def swap(source, target, ssem, rsem):
+        for d in range(1, GROUP):
+            within(source, target, ssem, rsem, d, q).start()
+        target[q] = source[q]
+        for d in range(1, GROUP):
+            within(source, target, ssem, rsem, d, lax.rem(q + GROUP - d, GROUP)).wait()
+
+    swap(s_ref, first, send1, recv1)
+    f32, bf16 = jnp.float32, jnp.bfloat16
+    zero = jnp.zeros(total.shape, f32)
+    member = lambda k: k + strand * (GROUP - 1 - 2 * k)
+    grow = [jnp.exp(log_ref[g * GROUP + member(k)]) for k in range(GROUP)]
+    added = [first[member(k)].astype(f32) for k in range(GROUP)]
+    state = zero
+    for k in range(GROUP):
+        state = grow[k] * state + added[k]
+    total[...] = state.astype(bf16)
+
+    def across(d, slot):
+        return remote(total, second.at[slot], send2.at[d], recv2.at[d], peer(d))
+
+    def start(d, _):
+        across(d, g).start()
+        return 0
+
+    def finish(d, _):
+        across(d, lax.rem(g + groups - d, groups)).wait()
+        return 0
+
+    lax.fori_loop(1, groups, start, 0)
+    second[g] = total[...]
+    lax.fori_loop(1, groups, finish, 0)
+    order = g + strand * (groups - 1 - 2 * g)
+
+    def earlier(k, state):
+        at = k + strand * (groups - 1 - 2 * k)
+        logs = log_ref[at * GROUP]
+        for i in range(1, GROUP):
+            logs = logs + log_ref[at * GROUP + i]
+        new = jnp.exp(logs) * state + second[at].astype(f32)
+        return jnp.where(k < order, new, state)
+
+    state = lax.fori_loop(0, groups, earlier, zero)
+    for k in range(GROUP):
+        third[member(k)] = state.astype(bf16)
+        state = grow[k] * state + added[k]
+    swap(third, landed, send3, recv3)
+    out_ref[...] = landed[...]
+
+
 def whole_spec(array):
     return pl.BlockSpec(array.shape, lambda *_: (0,) * array.ndim)
 
@@ -160,27 +307,42 @@
         ],
         axis=0,
     )
-    packed = lax.all_gather(packed, "ch", axis=1, tiled=True)
-    ow = lax.all_gather(out_weight, "ch", axis=0, tiled=True)
+    packed = jnp.pad(packed, ((0, 32 - packed.shape[0]), (0, 0)))
+
+    mine = lax.dynamic_slice_in_dim(tokens, ch * rows, rows, axis=1)
+    base = jnp.arange(5, dtype=jnp.int32)
+    counts = jnp.sum((mine[..., None] == base).astype(jnp.int32), axis=1)
+    info = jnp.concatenate([counts, mine[:, :3], mine[:, rows - 3 :]], axis=1)
+    info = jnp.pad(info, ((0, 8 - wins), (0, 128 - info.shape[1])))
+    vmem = pl.BlockSpec(memory_space=pltpu.VMEM)
+    dma = pltpu.SemaphoreType.DMA
+    tables = [
+        jax.ShapeDtypeStruct((devices,) + info.shape, jnp.int32),
+        jax.ShapeDtypeStruct((chs,) + packed.shape, f32),
+        jax.ShapeDtypeStruct((chs,) + out_weight.shape, bf16),
+    ]
+    info, packed, ow = pl.pallas_call(
+        partial(exchange_body, chs, devices),
+        in_specs=[vmem] * 3,
+        out_specs=[vmem] * 3,
+        out_shape=tables,
+        scratch_shapes=[pltpu.VMEM(v.shape, v.dtype) for v in tables]
+        + [dma((devices,))] * 2 + [dma((chs,))] * 4,
+        compiler_params=pltpu.CompilerParams(collective_id=0, has_side_effects=True),
+        name="exchange",
+    )(info, packed, out_weight)
+    packed = jnp.concatenate([packed[i] for i in range(chs)], axis=1)
+    ow = ow.reshape(chs * width, -1)
     inner_all, sg_all, step_all, ld_all = (packed[5 * i : 5 * i + 5] for i in range(4))
     taps_all, skip_all, gain_all = packed[20:24], packed[24:25], packed[25:26]
     tx = pieces(taps_all[:, None, :] * inner_all[None])
     tst = pieces(jnp.pad(state_kernel[:, None, :] * state_tab[None], ((0, 0), (0, 0), (0, 96))))
     tdt, tsg, ld = pieces(step_all[None]), pieces(sg_all[None]), pieces(ld_all[None])
 
-    halves = tokens.reshape(wins, chs, rows)
-    base = jnp.arange(5, dtype=jnp.int32)
-    counts = jnp.sum((halves[..., None] == base).astype(jnp.int32), axis=2)
-    info = jnp.concatenate(
-        [counts.reshape(wins, chs * 5), tokens[:, :3], tokens[:, held - 3 :]], axis=1
-    )
-    info = lax.all_gather(info, "seq")
     none = 7
-    edge = info[:, :, chs * 5 :]
-    before = jnp.where(seq > 0, edge[jnp.maximum(seq - 1, 0)][:, 3:], none)
-    after = jnp.where(seq < seqs - 1, edge[jnp.minimum(seq + 1, seqs - 1)][:, :3], none)
-    around = jnp.concatenate([before, tokens, after], axis=1)
-    mine = lax.dynamic_slice_in_dim(around, ch * rows, rows + 6, axis=1)
+    before = jnp.where(me > 0, info[jnp.maximum(me - 1, 0), :wins, 8:11], none)
+    after = jnp.where(me < devices - 1, info[jnp.minimum(me + 1, devices - 1), :wins, 5:8], none)
+    mine = jnp.concatenate([before, mine, after], axis=1)
     other = jnp.where(mine < 4, 3 - mine, mine)[:, ::-1]
     ids = jnp.stack([mine, other], axis=1).reshape(wins * 2, rows + 6)
     column = np.arange(COLS)
@@ -207,36 +369,44 @@
             row_spec(full),
             row_spec(128),
             pl.BlockSpec((1, subs, 16, full), lambda s, b: (s, b, 0, 0)),
-            pl.BlockSpec((1, 16, full), lambda s, b: (s, 0, 0)),
+            pl.BlockSpec((2, 16, full // 2), lambda s, b: (s, 0, 0)),
         ],
         out_shape=[
             jax.ShapeDtypeStruct((streams, rows, full), bf16),
             jax.ShapeDtypeStruct((streams, rows, 128), bf16),
             jax.ShapeDtypeStruct((streams, steps * subs, 16, full), f32),
-            jax.ShapeDtypeStruct((streams, 16, full), f32),
+            jax.ShapeDtypeStruct((streams * 2, 16, full // 2), bf16),
         ],
-        compiler_params=pltpu.CompilerParams(vmem_limit_bytes=40 << 20),
+        scratch_shapes=[pltpu.VMEM((16, full), f32)],
+        compiler_params=pltpu.CompilerParams(vmem_limit_bytes=56 << 20),
         name="states",
     )(onehot, tri, tx, tst, tdt, ld)
 
-    gathered = lax.all_gather(sfin.astype(bf16), ("seq", "ch"))
-    every = info[:, :, : chs * 5].reshape(seqs, wins, chs, 5)
-    every = jnp.moveaxis(every, 2, 1).reshape(devices, wins, 5).astype(f32)
-    j, m = np.arange(devices)[:, None], np.arange(devices)[None]
-    fwd = (j < m) & (m < me)
-    bwd = (j > m) & (m > me)
-    between = jnp.stack(
-        [
-            jnp.sum(jnp.where(fwd[..., None, None], every[None], 0.0), axis=1),
-            jnp.sum(jnp.where(bwd[..., None, None], every[None][..., jnp.array([3, 2, 1, 0, 4])], 0.0), axis=1),
-        ],
-        axis=2,
-    )
-    log_weight = jnp.sum(between[..., None] * ld_all, axis=3)
-    who = np.arange(devices)
-    reached = jnp.stack([who < me, who > me], axis=1)[:, None, :, None]
-    weight = jnp.where(reached, jnp.exp(log_weight), 0.0).reshape(devices, streams, 1, full)
-    incoming = jnp.sum(weight * gathered.astype(f32), axis=0)
+    q = lax.rem(me, GROUP)
+    window, strand, half = q // 4, (q // 2) % 2, q % 2
+    cnt = info[:, window, :5]
+    cnt = jnp.where(strand == 0, cnt, jnp.stack([cnt[:, i] for i in (3, 2, 1, 0, 4)], axis=1))
+    part = full // 2
+    ld_half = lax.dynamic_slice_in_dim(ld_all, half * part, part, axis=1)
+    logs = jnp.sum(cnt.astype(f32)[:, :, None] * ld_half[None], axis=1)[:, None, :]
+    groups = devices // GROUP
+    piece = (16, part)
+    incoming = pl.pallas_call(
+        partial(carry_body, chs, groups),
+        in_specs=[vmem] * 2,
+        out_specs=vmem,
+        out_shape=jax.ShapeDtypeStruct((GROUP,) + piece, bf16),
+        scratch_shapes=[
+            pltpu.VMEM((GROUP,) + piece, bf16),
+            pltpu.VMEM(piece, bf16),
+            pltpu.VMEM((groups,) + piece, bf16),
+            pltpu.VMEM((GROUP,) + piece, bf16),
+            pltpu.VMEM((GROUP,) + piece, bf16),
+        ]
+        + [dma((GROUP,))] * 2 + [dma((groups,))] * 2 + [dma((GROUP,))] * 2,
+        compiler_params=pltpu.CompilerParams(collective_id=1, has_side_effects=True),
+        name="carry",
+    )(sfin, logs)
 
     lane, t = np.arange(full)[None], np.arange(SUB)[:, None]
     causal = jnp.asarray(t >= lane % SUB, f32)
@@ -256,13 +426,13 @@
             stream((ROWS, full)),
             stream((ROWS, 128)),
             stream((subs, 16, full)),
-            pl.BlockSpec((1, 16, full), lambda w, s, b: (w * 2 + s, 0, 0)),
+            pl.BlockSpec((2, 16, full // 2), lambda w, s, b: (w * 2 + s, 0, 0)),
         ]
         + [whole_spec(v) for v in consts],
         out_specs=pl.BlockSpec((ROWS, model), lambda w, s, b: (steps - 1 - b * s, w)),
         out_shape=jax.ShapeDtypeStruct((rows, wins * model), bf16),
         scratch_shapes=[pltpu.VMEM((16, full), f32), pltpu.VMEM((rows, full), bf16)],
-        compiler_params=pltpu.CompilerParams(vmem_limit_bytes=40 << 20),
+        compiler_params=pltpu.CompilerParams(vmem_limit_bytes=56 << 20),
         name="outputs",
     )(onehot, x, kv, sloc, incoming, *consts)
     return out.reshape(rows, wins, model)

time: 164 us -> 98.1 us (0.60)
  waiting for transfers between devices: 45.3 us -> 0 us
  Pallas kernels: 36 us -> 72.8 us
  blocking collectives: 34.2 us -> 0 us
  between operations: 13.8 us -> 0.27 us
  local copies, waits for them, and re-layouts: 21.7 us -> 11.5 us
    all_gather x1 -> x0, waiting for transfers between devices: 45.3 us -> none  [on_device(): gathered = lax.all_gather(sfin.astype(bf16), ('seq', 'ch'))]
    all_gather x3 -> x0, blocking collectives: 34.2 us -> none  [the longest x1 22.2 us: on_device(): info = lax.all_gather(info, 'seq')]
    pallas_call x0 -> x2, Pallas kernels: none -> 30 us  [the longest x1 15.8 us: on_device(): pl.pallas_call(partial(exchange_body, chs, devices), in_specs=[vmem] * 3,...]
    unnamed x47 -> x13, local copies, waits for them, and re-layouts: 13.4 us -> 0.84 us
    pallas_call x1, Pallas kernels: 10.4 us -> 14.1 us  [on_device(): pl.pallas_call(state_kernel_body, grid=(streams, steps), in_specs=[row_sp...]
    pallas_call x1, Pallas kernels: 25.6 us -> 28.7 us  [on_device(): pl.pallas_call(output_kernel_body, grid=(wins, 2, steps), in_specs=[strea...]
    reduce_sum x5 -> x2, other arithmetic: 2.82 us -> 0.27 us  [the longest x1 0.18 us: on_device(): counts = jnp.sum((mine[..., None] == base).astype(jnp.int32), axis=1)]
    dynamic_slice x0 -> x4, local copies, waits for them, and re-layouts: none -> 1.72 us  [the longest x2 1 us: on_device(): cnt = info[:, window, :5]]
  transfers between devices with their start and end apart: 1 -> 0, of which waited for: 1 -> 0; matrix products, arithmetic and copies ran while one was open for 1% -> 0% of each run, Pallas kernels for 0% -> 0%
where the time goes in v2:
time: 98.1 us; the launch traced here: 96.6 us
  Pallas kernels  72.8 us (74%)
  local copies, waits for them, and re-layouts  11.5 us (12%)
  other arithmetic  8.52 us (9%)
  matrix products  3.58 us (4%)
    pallas_call x1, Pallas kernels, on_device(): pl.pallas_call(output_kernel_body, grid=(wins, 2, steps), in_specs=[strea...  28.7 us
    pallas_call x1, Pallas kernels, on_device(): pl.pallas_call(partial(exchange_body, chs, devices), in_specs=[vmem] * 3,...  15.8 us
    pallas_call x1, Pallas kernels, on_device(): pl.pallas_call(partial(carry_body, chs, groups), in_specs=[vmem] * 2, out...  14.1 us
    pallas_call x1, Pallas kernels, on_device(): pl.pallas_call(state_kernel_body, grid=(streams, steps), in_specs=[row_sp...  14.1 us
    convert_element_type x1, other arithmetic, on_device(): onehot = onehot.astype(bf16)  4.36 us
    dot_general x4, matrix products, dot(): return jnp.dot(a, b, preferred_element_type=jnp.float32)  3.58 us
    reshape x1, local copies, waits for them, and re-layouts, on_device(): return out.reshape(rows, wins, model)  2.13 us

profile of v2, /device:TPU:0, one launch (start us, length us, event | category | flops | bytes accessed | tf_op | source)
XLA Modules:
  0.0 96.6 jit_solution(16690850597158302006)
XLA Ops:
  0.2 0.8 constant_dynamic-slice_fusion
  1.0 0.7 broadcast_in_dim.25
  1.8 0.8 fusion.2
  2.6 0.8 negate_multiply_fusion
  3.5 0.1 copy.43
  3.6 0.1 copy.42
  3.9 0.1 reshape.98
  4.0 0.7 constant_dynamic-slice_fusion.6
  4.7 0.2 fusion.11
  4.9 0.1 copy.41
  5.0 0.6 pad.30.info_ref
  5.7 0.8 fusion.1
  6.5 1.1 %divide_multiply_fusion = f32[5,256]{1,0:T(8,128)S(1)} fusion(bf16[5,256]{1,0:T(8,128)(2,1)} %param.27, bf16[256,256]{1,0:T(8,128)(2,1)} %param.29), kind=kOutput, calls=%fused_computation.70 | convolution fusion | flops 663040 | bytes 138752 | tf_op jit(solution)/shard_map/dot_general | solution.py:37
  7.6 1.6 %concatenate.37 = f32[26,256]{1,0:T(8,128)S(1)} concatenate(f32[5,256]{1,0:T(8,128)S(1)} %fusion.1, f32[5,256]{1,0:T(8,128)S(1)} %divide_multiply_fusion, f32[5,256]{1,0:T(8,128)S(1)} %reshape.97, f32[5,256]{1,0:T(8,128)S(1)} %reshape.98, f32[4,256]{1,0:T(4,128)} %param.32, f32[1,256]{1,0:T(1,128)S(1)} %broadcast_in_dim_reshape.3, f32[1,256]{1,0:T(1,128)} %bitcast.72), dimensions={0} | concatenate | bytes 53248 | tf_op jit(solution)/shard_map/concatenate | solution.py:298
  9.1 0.6 pad.31.packed_ref
  9.8 0.7 broadcast_multiply_fusion.1
  10.5 0.7 maximum_maximum_fusion.4.tst_ref
  11.2 15.8 %exchange.1 = (s32[32,8,128]{2,1,0:T(8,128)}, f32[2,32,256]{2,1,0:T(8,128)}, bf16[2,256,256]{2,1,0:T(8,128)(2,1)}) custom-call(s32[8,128]{1,0:T(8,128)} %pad.30.info_ref, f32[32,256]{1,0:T(8,128)} %pad.31.packed_ref, bf16[256,256]{1,0:T(8,128)(2,1)} %ow_ref.1), custom_call_target="tpu_custom_call" | custom-call | tf_op jit(solution)/shard_map/exchange/pallas_call | solution.py:324
  27.0 0.8 slice_bitcast_fusion
  27.8 0.8 fusion.24
  28.5 0.9 constant_dynamic-slice_fusion.3
  29.5 0.1 concatenate.38
  29.7 0.6 pad_maximum_fusion.1
  30.3 0.8 reverse
  31.3 0.1 multiply_reduce_fusion
  31.4 0.6 broadcast_in_dim.31.log_ref
  32.2 1.0 %maximum_maximum_fusion.3 = (bf16[128,512]{1,0:T(8,128)(2,1)}, bf16[128,512]{1,0:T(8,128)(2,1)}, bf16[128,512]{1,0:T(8,128)(2,1)}, bf16[128,512]{1,0:T(8,128)(2,1)}) fusion(bf16[32,512]{1,0:T(8,128)(2,1)S(1)} %get-tuple-element.37, bf16[32,512]{1,0:T(8,128)(2,1)S(1)} %get-tuple-element.38, bf16[32,512]{1,0:T(8,128)(2,1)S(1)} %get-tuple-element.36, ...), kind=kLoop, calls=%fused_computation.12 | loop fusion | flops 1900544 | bytes 917760 | tf_op jit(solution)/shard_map/concatenate | solution.py:28
  33.2 4.4 %or_convert_fusion.oh_ref = bf16[4,1024,128]{2,1,0:T(8,128)(2,1)} fusion(s32[4,1024]{1,0:T(4,128)S(1)} %get-tuple-element.33, s32[4,1024]{1,0:T(4,128)S(1)} %get-tuple-element.34, s32[4,1024]{1,0:T(4,128)S(1)} %get-tuple-element.35, s32[128]{0:T(128)S(1)} %copy-done.5, s32[4,1024]{1,0:T(4,128)S(1)} %get-tuple-element.32, pred[128]{0:T(512)(128)(4,1)S(1)} %copy-done.1, ...), kind=kLoop, calls=%fused_computation | loop fusion | flops 6291456 | bytes 1115136 | tf_op jit(solution)/shard_map/convert_element_type | solution.py:354
  37.5 14.1 %states.1 = (bf16[4,1024,512]{2,1,0:T(8,128)(2,1)}, bf16[4,1024,128]{2,1,0:T(8,128)(2,1)}, f32[4,16,16,512]{3,2,1,0:T(8,128)}, bf16[8,16,256]{2,1,0:T(8,128)(2,1)}) custom-call(bf16[4,1024,128]{2,1,0:T(8,128)(2,1)} %or_convert_fusion.oh_ref, bf16[256,256]{1,0:T(8,128)(2,1)} %constant.110.clone.tri_ref, bf16[128,512]{1,0:T(8,128)(2,1)} %get-tuple-element.58.tx_ref, ...), custom_call_target="tpu_custom_call" | custom-call | tf_op jit(solution)/shard_map/states/pallas_call | solution.py:364
  51.7 14.1 %carry.1.inc_ref = bf16[8,16,256]{2,1,0:T(8,128)(2,1)} custom-call(bf16[8,16,256]{2,1,0:T(8,128)(2,1)} %get-tuple-element.17.s_ref, f32[32,1,256]{2,1,0:T(1,128)} %broadcast_in_dim.31.log_ref), custom_call_target="tpu_custom_call" | custom-call | tf_op jit(solution)/shard_map/carry/pallas_call | solution.py:394
  65.8 28.7 %outputs.1 = bf16[1024,512]{1,0:T(8,128)(2,1)} custom-call(bf16[4,1024,128]{2,1,0:T(8,128)(2,1)} %or_convert_fusion.oh_ref, bf16[4,1024,512]{2,1,0:T(8,128)(2,1)} %get-tuple-element.14.x_ref, bf16[4,1024,128]{2,1,0:T(8,128)(2,1)} %get-tuple-element.15.kv_ref, f32[4,16,16,512]{3,2,1,0:T(8,128)} %get-tuple-element.16.sloc_ref, ...), custom_call_target="tpu_custom_call" | custom-call | tf_op jit(solution)/shard_map/outputs/pallas_call | solution.py:421
  94.5 2.1 %reshape.106 = bf16[1024,2,256]{2,1,0:T(2,128)(2,1)} reshape(bf16[1024,512]{1,0:T(8,128)(2,1)} %outputs.1) | data formatting | bytes 2097152 | tf_op jit(solution)/shard_map/reshape | solution.py:438
  (36 shorter events, 0.9 us)
Async XLA Ops:
  0.0 5.7 %copy-start = (bf16[256,256]{1,0:T(8,128)(2,1)S(1)}, bf16[256,256]{1,0:T(8,128)(2,1)}, u32[]{:S(2)}) copy-start(bf16[256,256]{1,0:T(8,128)(2,1)} %param.28) | copy-start | bytes 393220
  0.0 33.1 %copy-start.1 = (pred[128]{0:T(512)(128)(4,1)S(1)}, pred[128]{0:T(512)(128)(4,1)}, u32[]{:S(2)}) copy-start(pred[128]{0:T(512)(128)(4,1)} %constant.109.clone) | copy-start | bytes 388
  0.0 33.1 %copy-start.2 = (pred[128]{0:T(512)(128)(4,1)S(1)}, pred[128]{0:T(512)(128)(4,1)}, u32[]{:S(2)}) copy-start(pred[128]{0:T(512)(128)(4,1)} %constant.108.clone) | copy-start | bytes 388
  0.0 33.1 %copy-start.3 = (pred[128]{0:T(512)(128)(4,1)S(1)}, pred[128]{0:T(512)(128)(4,1)}, u32[]{:S(2)}) copy-start(pred[128]{0:T(512)(128)(4,1)} %constant.107.clone) | copy-start | bytes 388
  0.0 33.1 %copy-start.4 = (pred[128]{0:T(512)(128)(4,1)S(1)}, pred[128]{0:T(512)(128)(4,1)}, u32[]{:S(2)}) copy-start(pred[128]{0:T(512)(128)(4,1)} %constant.106.clone) | copy-start | bytes 388
  0.0 33.1 %copy-start.5 = (s32[128]{0:T(128)S(1)}, s32[128]{0:T(128)}, u32[]{:S(2)}) copy-start(s32[128]{0:T(128)} %constant.105.clone) | copy-start | bytes 1540

commit v3 on v2

--- a/solution.py
+++ b/solution.py
@@ -14,21 +14,6 @@
 COLS = 128
 
 
-def split3(v):
-    hi = lax.reduce_precision(v, 8, 7)
-    rest = v - hi
-    mid = lax.reduce_precision(rest, 8, 7)
-    low = lax.reduce_precision(rest - mid, 8, 7)
-    return hi, mid, low
-
-
-def pieces(table):
-    taps, ids, width = table.shape
-    full = jnp.pad(table, ((0, 4 - taps), (0, 8 - ids), (0, 0))).reshape(32, width)
-    stacked = jnp.concatenate(split3(full) + (jnp.zeros_like(full),), axis=0)
-    return stacked.astype(jnp.bfloat16)
-
-
 def silu(v):
     return v * (1.0 / (1.0 + jnp.exp(-v)))
 
@@ -37,10 +22,11 @@
     return jnp.dot(a, b, preferred_element_type=jnp.float32)
 
 
-def state_kernel_body(oh_ref, tri_ref, tx_ref, tst_ref, tdt_ref, ld_ref, x_ref, kv_ref, sloc_ref, sfin_ref, state_ref):
+def state_kernel_body(oh_ref, tri_ref, tx_ref, tst_ref, tdt_ref, ld_ref, x_ref, kv_ref, sloc_ref, sfin_ref, state_ref, log_ref):
     @pl.when(pl.program_id(1) == 0)
     def _():
         state_ref[...] = jnp.zeros_like(state_ref)
+        log_ref[...] = jnp.zeros_like(log_ref)
 
     oh = oh_ref[0]
     x = silu(dot(oh, tx_ref[...])).astype(jnp.bfloat16)
@@ -49,11 +35,12 @@
     kv_ref[0] = kv
     cum = dot(dot(tri_ref[...], oh).astype(jnp.bfloat16), ld_ref[...])
     dt = dot(oh, tdt_ref[...])
-    state = state_ref[...]
+    state, log = state_ref[...], log_ref[...]
     for j in range(ROWS // SUB):
         rows = slice(j * SUB, (j + 1) * SUB)
         cum_j = cum[rows]
         tot = cum_j[SUB - 1 :]
+        log = log + tot
         wx = (x[rows].astype(jnp.float32) * dt[rows] * jnp.exp(tot - cum_j)).astype(jnp.bfloat16)
         new = lax.dot_general(
             kv[rows, :16], wx, (((0,), (0,)), ((), ())), preferred_element_type=jnp.float32
@@ -62,8 +49,11 @@
         state = jnp.exp(tot) * state + new
     state_ref[...] = state
     half = state.shape[1] // 2
-    sfin_ref[0] = state[:, :half].astype(jnp.bfloat16)
-    sfin_ref[1] = state[:, half:].astype(jnp.bfloat16)
+    log_ref[...] = log
+    for i in range(2):
+        lanes = slice(i * half, (i + 1) * half)
+        sfin_ref[i, 0:16, :] = state[:, lanes]
+        sfin_ref[i, 16:24, :] = jnp.broadcast_to(log[:, lanes], (8, half))
 
 
 def output_kernel_body(
@@ -132,22 +122,44 @@
 
 
 def exchange_body(
-    chs, devices, info_ref, packed_ref, ow_ref, info_out, packed_out, ow_out,
-    info_all, packed_all, ow_all, send, recv, psend, precv, osend, orecv,
+    chs, devices, rows, tokens_ref, emb_ref, iw_ref, gw_ref, sw_ref, stw_ref, ik_ref, sk_ref,
+    gain_ref, ow_ref, bias_ref, decay_ref, skip_ref,
+    tx_out, tst_out, tdt_out, tsg_out, ld_out, vec_out, ow_out, edge_out,
+    packed, packed_all, ow_all, own, edges, small, psend, precv, osend, orecv, esend, erecv,
 ):
+    f32, bf16 = jnp.float32, jnp.bfloat16
     seq, ch = lax.axis_index("seq"), lax.axis_index("ch")
     me = seq * chs + ch
     place = lambda d: (d // chs, lax.rem(d, chs))
+    after, before = place(lax.rem(me + 1, devices)), place(lax.rem(me + devices - 1, devices))
+    mate = lambda d: (seq, lax.rem(ch + d, chs))
     barrier = pltpu.get_barrier_semaphore()
-
-    def greet(d, _):
-        pl.semaphore_signal(
-            barrier, inc=1, device_id=place(lax.rem(me + d, devices)), device_id_type=MESH
-        )
-        return 0
-
-    lax.fori_loop(1, devices, greet, 0)
-    pl.semaphore_wait(barrier, devices - 1)
+    for device in [after, before] + [mate(d) for d in range(1, chs)]:
+        pl.semaphore_signal(barrier, inc=1, device_id=device, device_id_type=MESH)
+
+    wins = tokens_ref.shape[0]
+    own[...] = jnp.zeros_like(own)
+    own[0, :wins, :] = tokens_ref[:, pl.ds(pl.multiple_of(ch * rows, 128), 128)]
+    own[1, :wins, :] = tokens_ref[:, pl.ds(pl.multiple_of(ch * rows + rows - 128, 128), 128)]
+    width, heads = iw_ref.shape[1], stw_ref.shape[1]
+    emb = emb_ref[...]
+    packed[...] = jnp.zeros_like(packed)
+    packed[0:5, :] = dot(emb, iw_ref[...]).astype(bf16).astype(f32)
+    packed[8:13, :] = silu(dot(emb, gw_ref[...]).astype(bf16).astype(f32))
+    pre = dot(emb, stw_ref[...])
+    head = lax.broadcasted_iota(jnp.int32, (5, width), 1) // (width // heads)
+    raw, rate = jnp.zeros((5, width), f32), jnp.zeros((5, width), f32)
+    skip = jnp.zeros((5, width), f32)
+    for h in range(heads):
+        raw = jnp.where(head == h, pre[:, h : h + 1] + bias_ref[h], raw)
+        rate = jnp.where(head == h, decay_ref[h], rate)
+        skip = jnp.where(head == h, skip_ref[h], skip)
+    step = jnp.maximum(raw, 0.0) + jnp.log1p(jnp.exp(-jnp.abs(raw)))
+    packed[16:21, :] = step
+    packed[24:29, :] = -step * rate
+    packed[32:36, :] = ik_ref[...]
+    packed[40:41, :] = skip[0:1]
+    packed[41:42, :] = gain_ref[...]
 
     def remote(src, dst, ssem, rsem, device):
         return pltpu.make_async_remote_copy(
@@ -155,44 +167,55 @@
             device_id_type=MESH,
         )
 
-    def info_copy(d, slot):
-        return remote(
-            info_ref, info_all.at[slot], send.at[d], recv.at[d], place(lax.rem(me + d, devices))
+    def table_copies(d, slot):
+        return (
+            remote(packed, packed_all.at[slot], psend.at[d], precv.at[d], mate(d)),
+            remote(ow_ref, ow_all.at[slot], osend.at[d], orecv.at[d], mate(d)),
         )
 
-    def start(d, _):
-        info_copy(d, me).start()
-        return 0
-
-    def finish(d, _):
-        info_copy(d, lax.rem(me + devices - d, devices)).wait()
-        return 0
-
-    def table_copies(d, slot):
-        device = (seq, lax.rem(ch + d, chs))
-        return (
-            remote(packed_ref, packed_all.at[slot], psend.at[d], precv.at[d], device),
-            remote(ow_ref, ow_all.at[slot], osend.at[d], orecv.at[d], device),
-        )
-
+    edge_copies = (
+        remote(own.at[1], edges.at[0], esend.at[0], erecv.at[0], after),
+        remote(own.at[0], edges.at[1], esend.at[1], erecv.at[1], before),
+    )
+    pl.semaphore_wait(barrier, 1 + chs)
     for d in range(1, chs):
         for copy in table_copies(d, ch):
             copy.start()
-    lax.fori_loop(1, devices, start, 0)
-    info_all[me] = info_ref[...]
-    packed_all[ch] = packed_ref[...]
+    for copy in edge_copies:
+        copy.start()
+    packed_all[ch] = packed[...]
     ow_all[ch] = ow_ref[...]
+
+    def emit(ref, table):
+        hi = table.astype(bf16).astype(f32)
+        mid = (table - hi).astype(bf16).astype(f32)
+        low = table - hi - mid
+        ref[...] = jnp.concatenate([hi, mid, low, jnp.zeros_like(hi)], axis=0).astype(bf16)
+
+    small[...] = jnp.zeros_like(small)
+    state_tab = dot(emb, sw_ref[...]).astype(bf16).astype(f32)
+    for k in range(4):
+        small[8 * k : 8 * k + 5, : state_tab.shape[1]] = sk_ref[k : k + 1, :] * state_tab
+    emit(tst_out, small[...])
+    for copy in edge_copies:
+        copy.wait()
     for d in range(1, chs):
         for copy in table_copies(d, lax.rem(ch + chs - d, chs)):
             copy.wait()
-    lax.fori_loop(1, devices, finish, 0)
-    info_out[...] = info_all[...]
-    packed_out[...] = packed_all[...]
+    every = jnp.concatenate([packed_all[i] for i in range(chs)], axis=1)
+    zeros = jnp.zeros((24, width * chs), f32)
+    inner = every[0:8]
+    emit(tx_out, jnp.concatenate([every[32 + k : 33 + k] * inner for k in range(4)], axis=0))
+    emit(tsg_out, jnp.concatenate([every[8:16], zeros], axis=0))
+    emit(tdt_out, jnp.concatenate([every[16:24], zeros], axis=0))
+    emit(ld_out, jnp.concatenate([every[24:32], zeros], axis=0))
+    vec_out[...] = every[40:48]
     ow_out[...] = ow_all[...]
+    edge_out[...] = edges[...]
 
 
 def carry_body(
-    chs, groups, s_ref, log_ref, out_ref, first, total, second, third, landed,
+    chs, groups, s_ref, out_ref, first, total, second, third, landed,
     send1, recv1, send2, recv2, send3, recv3,
 ):
     me = lax.axis_index("seq") * chs + lax.axis_index("ch")
@@ -230,14 +253,16 @@
 
     swap(s_ref, first, send1, recv1)
     f32, bf16 = jnp.float32, jnp.bfloat16
-    zero = jnp.zeros(total.shape, f32)
+    zero = jnp.zeros(out_ref.shape[1:], f32)
     member = lambda k: k + strand * (GROUP - 1 - 2 * k)
-    grow = [jnp.exp(log_ref[g * GROUP + member(k)]) for k in range(GROUP)]
-    added = [first[member(k)].astype(f32) for k in range(GROUP)]
+    logs = [first[member(k), 16:17, :] for k in range(GROUP)]
+    grow = [jnp.exp(log) for log in logs]
+    added = [first[member(k), 0:16, :] for k in range(GROUP)]
     state = zero
     for k in range(GROUP):
         state = grow[k] * state + added[k]
-    total[...] = state.astype(bf16)
+    total[0:16, :] = state
+    total[16:24, :] = jnp.broadcast_to(sum(logs), (8, state.shape[1]))
 
     def across(d, slot):
         return remote(total, second.at[slot], send2.at[d], recv2.at[d], peer(d))
@@ -257,10 +282,7 @@
 
     def earlier(k, state):
         at = k + strand * (groups - 1 - 2 * k)
-        logs = log_ref[at * GROUP]
-        for i in range(1, GROUP):
-            logs = logs + log_ref[at * GROUP + i]
-        new = jnp.exp(logs) * state + second[at].astype(f32)
+        new = jnp.exp(second[at, 16:17, :]) * state + second[at, 0:16, :]
         return jnp.where(k < order, new, state)
 
     state = lax.fori_loop(0, groups, earlier, zero)
@@ -290,58 +312,40 @@
     width = inner_weight.shape[1]
     head_width = width // heads_here
 
-    inner_tab = dot(embedding, inner_weight).astype(bf16).astype(f32)
-    gate_tab = dot(embedding, gate_weight).astype(bf16).astype(f32)
-    state_tab = dot(embedding, state_weight).astype(bf16).astype(f32)
-    step_tab = jax.nn.softplus(dot(embedding, step_weight) + step_bias)
-    spread = lambda v: jnp.repeat(v, head_width, axis=-1)
-    packed = jnp.concatenate(
-        [
-            inner_tab,
-            jax.nn.silu(gate_tab),
-            spread(step_tab),
-            spread(-step_tab * decay_rates),
-            inner_kernel,
-            spread(skip_gain)[None],
-            norm_gain[None],
+    full, model = width * chs, out_weight.shape[1]
+    vmem, smem = (pl.BlockSpec(memory_space=m) for m in (pltpu.VMEM, pltpu.SMEM))
+    dma = pltpu.SemaphoreType.DMA
+    shape = jax.ShapeDtypeStruct
+    table = shape((COLS, full), bf16)
+    tx, tst, tdt, tsg, ld, vec, ow, edge = pl.pallas_call(
+        partial(exchange_body, chs, devices, rows),
+        in_specs=[vmem] * 10 + [smem] * 3,
+        out_specs=[vmem] * 8,
+        out_shape=[
+            table, shape((COLS, 128), bf16), table, table, table, shape((8, full), f32),
+            shape((chs, width, model), bf16), shape((2, 8, 128), jnp.int32),
         ],
-        axis=0,
-    )
-    packed = jnp.pad(packed, ((0, 32 - packed.shape[0]), (0, 0)))
-
-    mine = lax.dynamic_slice_in_dim(tokens, ch * rows, rows, axis=1)
-    base = jnp.arange(5, dtype=jnp.int32)
-    counts = jnp.sum((mine[..., None] == base).astype(jnp.int32), axis=1)
-    info = jnp.concatenate([counts, mine[:, :3], mine[:, rows - 3 :]], axis=1)
-    info = jnp.pad(info, ((0, 8 - wins), (0, 128 - info.shape[1])))
-    vmem = pl.BlockSpec(memory_space=pltpu.VMEM)
-    dma = pltpu.SemaphoreType.DMA
-    tables = [
-        jax.ShapeDtypeStruct((devices,) + info.shape, jnp.int32),
-        jax.ShapeDtypeStruct((chs,) + packed.shape, f32),
-        jax.ShapeDtypeStruct((chs,) + out_weight.shape, bf16),
-    ]
-    info, packed, ow = pl.pallas_call(
-        partial(exchange_body, chs, devices),
-        in_specs=[vmem] * 3,
-        out_specs=[vmem] * 3,
-        out_shape=tables,
-        scratch_shapes=[pltpu.VMEM(v.shape, v.dtype) for v in tables]
-        + [dma((devices,))] * 2 + [dma((chs,))] * 4,
+        scratch_shapes=[
+            pltpu.VMEM((48, width), f32),
+            pltpu.VMEM((chs, 48, width), f32),
+            pltpu.VMEM((chs, width, model), bf16),
+            pltpu.VMEM((2, 8, 128), jnp.int32),
+            pltpu.VMEM((2, 8, 128), jnp.int32),
+            pltpu.VMEM((32, 128), f32),
+        ]
+        + [dma((chs,))] * 4 + [dma((2,))] * 2,
         compiler_params=pltpu.CompilerParams(collective_id=0, has_side_effects=True),
         name="exchange",
-    )(info, packed, out_weight)
-    packed = jnp.concatenate([packed[i] for i in range(chs)], axis=1)
-    ow = ow.reshape(chs * width, -1)
-    inner_all, sg_all, step_all, ld_all = (packed[5 * i : 5 * i + 5] for i in range(4))
-    taps_all, skip_all, gain_all = packed[20:24], packed[24:25], packed[25:26]
-    tx = pieces(taps_all[:, None, :] * inner_all[None])
-    tst = pieces(jnp.pad(state_kernel[:, None, :] * state_tab[None], ((0, 0), (0, 0), (0, 96))))
-    tdt, tsg, ld = pieces(step_all[None]), pieces(sg_all[None]), pieces(ld_all[None])
-
+    )(
+        tokens, embedding, inner_weight, gate_weight, state_weight, step_weight, inner_kernel,
+        state_kernel, norm_gain[None], out_weight, step_bias, decay_rates, skip_gain,
+    )
+    ow = ow.reshape(full, model)
+    skip_all, gain_all = vec[0:1], vec[1:2]
+    mine = lax.dynamic_slice_in_dim(tokens, ch * rows, rows, axis=1)
     none = 7
-    before = jnp.where(me > 0, info[jnp.maximum(me - 1, 0), :wins, 8:11], none)
-    after = jnp.where(me < devices - 1, info[jnp.minimum(me + 1, devices - 1), :wins, 5:8], none)
+    before = jnp.where(me > 0, edge[0, :wins, 125:], none)
+    after = jnp.where(me < devices - 1, edge[1, :wins, :3], none)
     mine = jnp.concatenate([before, mine, after], axis=1)
     other = jnp.where(mine < 4, 3 - mine, mine)[:, ::-1]
     ids = jnp.stack([mine, other], axis=1).reshape(wins * 2, rows + 6)
@@ -355,7 +359,6 @@
 
     streams, steps = wins * 2, rows // ROWS
     subs = ROWS // SUB
-    full = width * chs
     index = np.arange(ROWS)
     tri = jnp.asarray(
         (index[:, None] >= index[None]) & (index[:, None] // SUB == index[None] // SUB), bf16
@@ -369,44 +372,37 @@
             row_spec(full),
             row_spec(128),
             pl.BlockSpec((1, subs, 16, full), lambda s, b: (s, b, 0, 0)),
-            pl.BlockSpec((2, 16, full // 2), lambda s, b: (s, 0, 0)),
+            pl.BlockSpec((2, 24, full // 2), lambda s, b: (s, 0, 0)),
         ],
         out_shape=[
             jax.ShapeDtypeStruct((streams, rows, full), bf16),
             jax.ShapeDtypeStruct((streams, rows, 128), bf16),
             jax.ShapeDtypeStruct((streams, steps * subs, 16, full), f32),
-            jax.ShapeDtypeStruct((streams * 2, 16, full // 2), bf16),
+            jax.ShapeDtypeStruct((streams * 2, 24, full // 2), f32),
         ],
-        scratch_shapes=[pltpu.VMEM((16, full), f32)],
+        scratch_shapes=[pltpu.VMEM((16, full), f32), pltpu.VMEM((1, full), f32)],
         compiler_params=pltpu.CompilerParams(vmem_limit_bytes=56 << 20),
         name="states",
     )(onehot, tri, tx, tst, tdt, ld)
 
-    q = lax.rem(me, GROUP)
-    window, strand, half = q // 4, (q // 2) % 2, q % 2
-    cnt = info[:, window, :5]
-    cnt = jnp.where(strand == 0, cnt, jnp.stack([cnt[:, i] for i in (3, 2, 1, 0, 4)], axis=1))
-    part = full // 2
-    ld_half = lax.dynamic_slice_in_dim(ld_all, half * part, part, axis=1)
-    logs = jnp.sum(cnt.astype(f32)[:, :, None] * ld_half[None], axis=1)[:, None, :]
     groups = devices // GROUP
-    piece = (16, part)
+    piece, message = (16, full // 2), (24, full // 2)
     incoming = pl.pallas_call(
         partial(carry_body, chs, groups),
-        in_specs=[vmem] * 2,
+        in_specs=[vmem],
         out_specs=vmem,
         out_shape=jax.ShapeDtypeStruct((GROUP,) + piece, bf16),
         scratch_shapes=[
-            pltpu.VMEM((GROUP,) + piece, bf16),
-            pltpu.VMEM(piece, bf16),
-            pltpu.VMEM((groups,) + piece, bf16),
+            pltpu.VMEM((GROUP,) + message, f32),
+            pltpu.VMEM(message, f32),
+            pltpu.VMEM((groups,) + message, f32),
             pltpu.VMEM((GROUP,) + piece, bf16),
             pltpu.VMEM((GROUP,) + piece, bf16),
         ]
         + [dma((GROUP,))] * 2 + [dma((groups,))] * 2 + [dma((GROUP,))] * 2,
         compiler_params=pltpu.CompilerParams(collective_id=1, has_side_effects=True),
         name="carry",
-    )(sfin, logs)
+    )(sfin)
 
     lane, t = np.arange(full)[None], np.arange(SUB)[:, None]
     causal = jnp.asarray(t >= lane % SUB, f32)
@@ -417,7 +413,6 @@
         (1,) + shape, lambda w, s, b: (w * 2 + s, b) + (0,) * (len(shape) - 1)
     )
     consts = (tri, tdt, tsg, ld, skip_all, gain_all, ow, causal, diag, bd, flip)
-    model = out_weight.shape[1]
     out = pl.pallas_call(
         output_kernel_body,
         grid=(wins, 2, steps),

time: 98.1 us -> 86.5 us (0.88)
  matrix products: 3.58 us -> 0 us
  local copies, waits for them, and re-layouts: 11.5 us -> 8.19 us
  other arithmetic: 8.52 us -> 5.87 us
  Pallas kernels: 72.8 us -> 71.2 us
    dot_general x4 -> x0, matrix products: 3.58 us -> none  [dot(): return jnp.dot(a, b, preferred_element_type=jnp.float32)]
    unnamed x13 -> x3, local copies, waits for them, and re-layouts: 0.84 us -> 3.68 us
    concatenate x4 -> x0, other arithmetic: 2.35 us -> none  [the longest x2 1.68 us: pieces(): stacked = jnp.concatenate(split3(full) + (jnp.zeros_like(full),), axis=0)]
    pallas_call x2, Pallas kernels: 30 us -> 28.3 us  [the longest x1 16.6 us: on_device(): pl.pallas_call(partial(carry_body, chs, groups), in_specs=[vmem], out_spe...]
    concatenate x2 -> x0, local copies, waits for them, and re-layouts: 1.67 us -> none  [the longest x1 1.59 us: on_device(): jnp.concatenate([inner_tab, jax.nn.silu(gate_tab), spread(step_tab), spre...]
    broadcast_in_dim x4 -> x0, local copies, waits for them, and re-layouts: 1.51 us -> none  [the longest x3 0.87 us: on_device(): spread = lambda v: jnp.repeat(v, head_width, axis=-1)]
    pad x2 -> x0, local copies, waits for them, and re-layouts: 1.22 us -> none  [the longest x1 0.62 us: on_device(): packed = jnp.pad(packed, ((0, 32 - packed.shape[0]), (0, 0)))]
    dynamic_slice x3 -> x0, local copies, waits for them, and re-layouts: 1.01 us -> none  [the longest x2 1 us: on_device(): cnt = info[:, window, :5]]
where the time goes in v3:
time: 86.5 us; the launch traced here: 85.3 us
  Pallas kernels  71.2 us (82%)
  local copies, waits for them, and re-layouts  8.19 us (9%)
  other arithmetic  5.87 us (7%)
    pallas_call x1, Pallas kernels, on_device(): pl.pallas_call(output_kernel_body, grid=(wins, 2, steps), in_specs=[strea...  28.7 us
    pallas_call x1, Pallas kernels, on_device(): pl.pallas_call(partial(carry_body, chs, groups), in_specs=[vmem], out_spe...  16.6 us
    pallas_call x1, Pallas kernels, on_device(): pl.pallas_call(state_kernel_body, grid=(streams, steps), in_specs=[row_sp...  14.2 us
    pallas_call x1, Pallas kernels, on_device(): pl.pallas_call(partial(exchange_body, chs, devices, rows), in_specs=[vmem...  11.7 us
    convert_element_type x1, other arithmetic, on_device(): onehot = onehot.astype(bf16)  5.1 us
    unnamed x3, local copies, waits for them, and re-layouts  3.68 us
    reshape x1, local copies, waits for them, and re-layouts, on_device(): return out.reshape(rows, wins, model)  2.13 us

profile of v3, /device:TPU:0, one launch (start us, length us, event | category | flops | bytes accessed | tf_op | source)
XLA Modules:
  0.0 85.3 jit_solution(10075840204205799349)
XLA Ops:
  0.0 0.7 constant_dynamic-slice_fusion
  0.7 1.4 %copy.29.sw_ref = bf16[256,32]{1,0:T(8,128)(2,1)} copy(bf16[256,32]{0,1:T(8,128)(2,1)} %param.30) | data formatting | bytes 32768 | tf_op args[4]
  2.1 1.4 %copy.30.stw_ref = bf16[256,4]{1,0:T(8,128)(2,1)} copy(bf16[256,4]{0,1:T(4,128)(2,1)} %param.31) | data formatting | bytes 4096 | tf_op args[5]
  3.6 11.7 %exchange.1 = (bf16[128,512]{1,0:T(8,128)(2,1)}, bf16[128,128]{1,0:T(8,128)(2,1)}, bf16[128,512]{1,0:T(8,128)(2,1)}, bf16[128,512]{1,0:T(8,128)(2,1)}, bf16[128,...) custom-call(s32[2,2048]{1,0:T(2,128)} %tokens_ref.1, ...), custom_call_target="tpu_custom_call" | custom-call | tf_op jit(solution)/shard_map/exchange/pallas_call | solution.py:320
  15.3 0.8 select_bitcast_fusion
  16.1 0.1 concatenate.3
  16.2 1.4 %fusion.1 = (f32[1,512]{1,0:T(1,128)}, f32[1,512]{1,0:T(1,128)}) fusion(f32[8,512]{1,0:T(8,128)} %get-tuple-element.27), kind=kLoop, calls=%fused_computation.7 | loop fusion | bytes 8192 | tf_op jit(solution)/shard_map/slice | solution.py:344
  17.6 0.8 reverse
  18.4 0.1 slice_bitcast_fusion
  18.5 0.1 fusion
  18.6 5.1 %or_convert_fusion.oh_ref = bf16[4,1024,128]{2,1,0:T(8,128)(2,1)} fusion(s32[4,1024]{1,0:T(4,128)S(1)} %get-tuple-element.30, s32[4,1024]{1,0:T(4,128)S(1)} %get-tuple-element.31, s32[4,1024]{1,0:T(4,128)S(1)} %get-tuple-element.32, s32[128]{0:T(128)} %constant.44.clone, s32[4,1024]{1,0:T(4,128)S(1)} %get-tuple-element.29, pred[128]{0:T(512)(128)(4,1)} %constant.48.clone, ...), kind=kLoop, calls=%fused_computation | loop fusion | flops 6291456 | bytes 1115136 | tf_op jit(solution)/shard_map/convert_element_type | solution.py:358
  23.7 14.2 %states.1 = (bf16[4,1024,512]{2,1,0:T(8,128)(2,1)}, bf16[4,1024,128]{2,1,0:T(8,128)(2,1)}, f32[4,16,16,512]{3,2,1,0:T(8,128)}, f32[8,24,256]{2,1,0:T(8,128)}) custom-call(bf16[4,1024,128]{2,1,0:T(8,128)(2,1)} %or_convert_fusion.oh_ref, bf16[256,256]{1,0:T(8,128)(2,1)} %constant.49.clone.tri_ref, bf16[128,512]{1,0:T(8,128)(2,1)} %get-tuple-element.18.tx_ref, ...), custom_call_target="tpu_custom_call" | custom-call | tf_op jit(solution)/shard_map/states/pallas_call | solution.py:367
  37.9 16.6 %carry.1.inc_ref = bf16[8,16,256]{2,1,0:T(8,128)(2,1)} custom-call(f32[8,24,256]{2,1,0:T(8,128)} %get-tuple-element.25.s_ref), custom_call_target="tpu_custom_call" | custom-call | tf_op jit(solution)/shard_map/carry/pallas_call | solution.py:390
  54.4 28.7 %outputs.1 = bf16[1024,512]{1,0:T(8,128)(2,1)} custom-call(bf16[4,1024,128]{2,1,0:T(8,128)(2,1)} %or_convert_fusion.oh_ref, bf16[4,1024,512]{2,1,0:T(8,128)(2,1)} %get-tuple-element.22.x_ref, bf16[4,1024,128]{2,1,0:T(8,128)(2,1)} %get-tuple-element.23.kv_ref, f32[4,16,16,512]{3,2,1,0:T(8,128)} %get-tuple-element.24.sloc_ref, ...), custom_call_target="tpu_custom_call" | custom-call | tf_op jit(solution)/shard_map/outputs/pallas_call | solution.py:416
  83.1 2.1 %reshape.29 = bf16[1024,2,256]{2,1,0:T(2,128)(2,1)} reshape(bf16[1024,512]{1,0:T(8,128)(2,1)} %outputs.1) | data formatting | bytes 2097152 | tf_op jit(solution)/shard_map/reshape | solution.py:433
  (4 shorter events, 0.0 us)

commit v4 on v3

--- a/solution.py
+++ b/solution.py
@@ -9,7 +9,8 @@
 from jax.sharding import PartitionSpec as P
 
 SUB = 64
-ROWS = 256
+ROWS = 1024
+TRI = 256
 EPS = 1e-05
 COLS = 128
 
@@ -18,22 +19,36 @@
     return v * (1.0 / (1.0 + jnp.exp(-v)))
 
 
+def dot_t(a, b):
+    return lax.dot_general(a, b, (((1,), (1,)), ((), ())), preferred_element_type=jnp.float32)
+
+
 def dot(a, b):
     return jnp.dot(a, b, preferred_element_type=jnp.float32)
 
 
-def state_kernel_body(oh_ref, tri_ref, tx_ref, tst_ref, tdt_ref, ld_ref, x_ref, kv_ref, sloc_ref, sfin_ref, state_ref, log_ref):
+def logs_of(tri, oh, ld):
+    counts = [dot(tri, oh[i : i + TRI]).astype(jnp.bfloat16) for i in range(0, ROWS, TRI)]
+    return dot(jnp.concatenate(counts, axis=0), ld)
+
+
+def state_kernel_body(ids_ref, tri_ref, tx_ref, tst_ref, tdt_ref, ld_ref, oh_ref, x_ref, kv_ref, sloc_ref, sfin_ref, state_ref, log_ref):
     @pl.when(pl.program_id(1) == 0)
     def _():
         state_ref[...] = jnp.zeros_like(state_ref)
         log_ref[...] = jnp.zeros_like(log_ref)
 
-    oh = oh_ref[0]
+    ids = ids_ref[0]
+    base = lax.broadcasted_iota(jnp.int32, (8, ROWS), 0)
+    hits = [jnp.where(ids[k : k + 1] == base, 1.0, 0.0) for k in range(4)]
+    rest = jnp.zeros((COLS - 96, ROWS), jnp.float32)
+    oh = jnp.concatenate(hits * 3 + [rest], axis=0).T.astype(jnp.bfloat16)
+    oh_ref[0] = oh
     x = silu(dot(oh, tx_ref[...])).astype(jnp.bfloat16)
     x_ref[0] = x
     kv = silu(dot(oh, tst_ref[...])).astype(jnp.bfloat16)
     kv_ref[0] = kv
-    cum = dot(dot(tri_ref[...], oh).astype(jnp.bfloat16), ld_ref[...])
+    cum = logs_of(tri_ref[...], oh, ld_ref[...])
     dt = dot(oh, tdt_ref[...])
     state, log = state_ref[...], log_ref[...]
     for j in range(ROWS // SUB):
@@ -69,7 +84,7 @@
         state_ref[...] = jnp.concatenate([inc_ref[0], inc_ref[1]], axis=1).astype(jnp.float32)
 
     oh = oh_ref[0]
-    cum = dot(dot(tri_ref[...], oh).astype(jnp.bfloat16), ld_ref[...])
+    cum = logs_of(tri_ref[...], oh, ld_ref[...])
     dt = dot(oh, tdt_ref[...])
     sg = dot(oh, tsg_ref[...])
     skip, gain = skip_ref[...], gain_ref[...]
@@ -110,7 +125,9 @@
 
     @pl.when(strand == 1)
     def _():
-        back = dot(flip_ref[...], normed).astype(jnp.bfloat16)
+        back = jnp.concatenate(
+            [dot(flip_ref[...], normed[i : i + TRI]) for i in range(ROWS - TRI, -1, -TRI)], axis=0
+        ).astype(jnp.bfloat16)
         start = pl.multiple_of((count - 1 - sb) * ROWS, ROWS)
         front = front_ref[pl.ds(start, ROWS), :]
         ow = ow_ref[...]
@@ -141,12 +158,12 @@
     own[...] = jnp.zeros_like(own)
     own[0, :wins, :] = tokens_ref[:, pl.ds(pl.multiple_of(ch * rows, 128), 128)]
     own[1, :wins, :] = tokens_ref[:, pl.ds(pl.multiple_of(ch * rows + rows - 128, 128), 128)]
-    width, heads = iw_ref.shape[1], stw_ref.shape[1]
+    width, heads = iw_ref.shape[1], stw_ref.shape[0]
     emb = emb_ref[...]
     packed[...] = jnp.zeros_like(packed)
     packed[0:5, :] = dot(emb, iw_ref[...]).astype(bf16).astype(f32)
     packed[8:13, :] = silu(dot(emb, gw_ref[...]).astype(bf16).astype(f32))
-    pre = dot(emb, stw_ref[...])
+    pre = dot_t(emb, stw_ref[...])
     head = lax.broadcasted_iota(jnp.int32, (5, width), 1) // (width // heads)
     raw, rate = jnp.zeros((5, width), f32), jnp.zeros((5, width), f32)
     skip = jnp.zeros((5, width), f32)
@@ -193,7 +210,7 @@
         ref[...] = jnp.concatenate([hi, mid, low, jnp.zeros_like(hi)], axis=0).astype(bf16)
 
     small[...] = jnp.zeros_like(small)
-    state_tab = dot(emb, sw_ref[...]).astype(bf16).astype(f32)
+    state_tab = dot_t(emb, sw_ref[...]).astype(bf16).astype(f32)
     for k in range(4):
         small[8 * k : 8 * k + 5, : state_tab.shape[1]] = sk_ref[k : k + 1, :] * state_tab
     emit(tst_out, small[...])
@@ -337,7 +354,7 @@
         compiler_params=pltpu.CompilerParams(collective_id=0, has_side_effects=True),
         name="exchange",
     )(
-        tokens, embedding, inner_weight, gate_weight, state_weight, step_weight, inner_kernel,
+        tokens, embedding, inner_weight, gate_weight, state_weight.T, step_weight.T, inner_kernel,
         state_kernel, norm_gain[None], out_weight, step_bias, decay_rates, skip_gain,
     )
     ow = ow.reshape(full, model)
@@ -349,32 +366,29 @@
     mine = jnp.concatenate([before, mine, after], axis=1)
     other = jnp.where(mine < 4, 3 - mine, mine)[:, ::-1]
     ids = jnp.stack([mine, other], axis=1).reshape(wins * 2, rows + 6)
-    column = np.arange(COLS)
-    tap_of, id_of = (column // 8) % 4, column % 8
-    onehot = jnp.zeros((wins * 2, rows, COLS), jnp.bool_)
-    for k in range(4):
-        tap = ids[:, 3 - k : 3 - k + rows, None] == jnp.asarray(id_of, jnp.int32)
-        onehot = onehot | (tap & jnp.asarray(tap_of == k))
-    onehot = onehot.astype(bf16)
+    taps = jnp.stack([ids[:, 3 - k : 3 - k + rows] for k in range(4)], axis=1)
+    taps = jnp.pad(taps, ((0, 0), (0, 4), (0, 0)), constant_values=none)
 
     streams, steps = wins * 2, rows // ROWS
     subs = ROWS // SUB
-    index = np.arange(ROWS)
+    index = np.arange(TRI)
     tri = jnp.asarray(
         (index[:, None] >= index[None]) & (index[:, None] // SUB == index[None] // SUB), bf16
     )
     row_spec = lambda n: pl.BlockSpec((1, ROWS, n), lambda s, b: (s, b, 0))
-    x, kv, sloc, sfin = pl.pallas_call(
+    onehot, x, kv, sloc, sfin = pl.pallas_call(
         state_kernel_body,
         grid=(streams, steps),
-        in_specs=[row_spec(COLS)] + [whole_spec(v) for v in (tri, tx, tst, tdt, ld)],
+        in_specs=[pl.BlockSpec((1, 8, ROWS), lambda s, b: (s, 0, b))] + [whole_spec(v) for v in (tri, tx, tst, tdt, ld)],
         out_specs=[
+            row_spec(COLS),
             row_spec(full),
             row_spec(128),
             pl.BlockSpec((1, subs, 16, full), lambda s, b: (s, b, 0, 0)),
             pl.BlockSpec((2, 24, full // 2), lambda s, b: (s, 0, 0)),
         ],
         out_shape=[
+            jax.ShapeDtypeStruct((streams, rows, COLS), bf16),
             jax.ShapeDtypeStruct((streams, rows, full), bf16),
             jax.ShapeDtypeStruct((streams, rows, 128), bf16),
             jax.ShapeDtypeStruct((streams, steps * subs, 16, full), f32),
@@ -383,7 +397,7 @@
         scratch_shapes=[pltpu.VMEM((16, full), f32), pltpu.VMEM((1, full), f32)],
         compiler_params=pltpu.CompilerParams(vmem_limit_bytes=56 << 20),
         name="states",
-    )(onehot, tri, tx, tst, tdt, ld)
+    )(taps, tri, tx, tst, tdt, ld)
 
     groups = devices // GROUP
     piece, message = (16, full // 2), (24, full // 2)
@@ -408,7 +422,7 @@
     causal = jnp.asarray(t >= lane % SUB, f32)
     diag = jnp.asarray(t == lane % SUB, f32)
     bd = jnp.asarray(np.arange(256)[:, None] // 64 == np.arange(256)[None] // 64, bf16)
-    flip = jnp.asarray(np.eye(ROWS)[::-1], bf16)
+    flip = jnp.asarray(np.eye(TRI)[::-1], bf16)
     stream = lambda shape: pl.BlockSpec(
         (1,) + shape, lambda w, s, b: (w * 2 + s, b) + (0,) * (len(shape) - 1)
     )

time: 86.5 us -> 66.4 us (0.77)
  Pallas kernels: 71.2 us -> 58.9 us
  other arithmetic: 5.87 us -> 0.84 us
  local copies, waits for them, and re-layouts: 8.19 us -> 6.04 us
    pallas_call x1, Pallas kernels: 28.7 us -> 21.5 us  [on_device(): pl.pallas_call(output_kernel_body, grid=(wins, 2, steps), in_specs=[strea...]
    convert_element_type x1 -> x0, other arithmetic: 5.1 us -> none  [on_device(): onehot = onehot.astype(bf16)]
    pallas_call x1, Pallas kernels: 14.2 us -> 9.25 us  [on_device(): pl.pallas_call(state_kernel_body, grid=(streams, steps), in_specs=[pl.Blo...]
    unnamed x3 -> x1, local copies, waits for them, and re-layouts: 3.68 us -> 0.81 us
where the time goes in v4:
time: 66.4 us; the launch traced here: 65.9 us
  Pallas kernels  58.9 us (89%)
  local copies, waits for them, and re-layouts  6.04 us (9%)
  other arithmetic  0.84 us (1%)
    pallas_call x1, Pallas kernels, on_device(): pl.pallas_call(output_kernel_body, grid=(wins, 2, steps), in_specs=[strea...  21.5 us
    pallas_call x1, Pallas kernels, on_device(): pl.pallas_call(partial(carry_body, chs, groups), in_specs=[vmem], out_spe...  16.6 us
    pallas_call x1, Pallas kernels, on_device(): pl.pallas_call(partial(exchange_body, chs, devices, rows), in_specs=[vmem...  11.7 us
    pallas_call x1, Pallas kernels, on_device(): pl.pallas_call(state_kernel_body, grid=(streams, steps), in_specs=[pl.Blo...  9.25 us
    reshape x1, local copies, waits for them, and re-layouts, on_device(): return out.reshape(rows, wins, model)  2.13 us
    slice x1, local copies, waits for them, and re-layouts, on_device(): skip_all, gain_all = (vec[0:1], vec[1:2])  1.39 us

profile of v4, /device:TPU:0, one launch (start us, length us, event | category | flops | bytes accessed | tf_op | source)
XLA Modules:
  0.0 65.9 jit_solution(16313977160483478807)
XLA Ops:
  0.0 0.7 %constant_dynamic-slice_fusion = s32[2,1024]{1,0:T(2,128)S(1)} fusion(s32[2,2048]{1,0:T(2,128)} %tokens_ref.1, s32[]{:T(128)S(6)} %select_n.30), kind=kLoop, calls=%fused_computation.8 | loop fusion | bytes 16388 | tf_op jit(solution)/shard_map/dynamic_slice | solution.py:362
  0.7 11.7 %exchange.1 = (bf16[128,512]{1,0:T(8,128)(2,1)}, bf16[128,128]{1,0:T(8,128)(2,1)}, bf16[128,512]{1,0:T(8,128)(2,1)}, bf16[128,512]{1,0:T(8,128)(2,1)}, bf16[128,...) custom-call(s32[2,2048]{1,0:T(2,128)} %tokens_ref.1, ...), custom_call_target="tpu_custom_call" | custom-call | tf_op jit(solution)/shard_map/exchange/pallas_call | solution.py:337
  12.4 0.8 %select_bitcast_fusion = (s32[2,3]{1,0:T(2,128)S(1)}, s32[2,3]{1,0:T(2,128)S(1)}) fusion(s32[2,8,128]{2,1,0:T(8,128)} %get-tuple-element.18, pred[]{:T(512)S(6)} %lt.13, pred[]{:T(512)S(6)} %gt.3), kind=kLoop, calls=%fused_computation.6 | loop fusion | flops 12 | bytes 98 | tf_op jit(solution)/shard_map/jit(_where)/select_n | solution.py:365
  13.1 0.1 concatenate.3
  13.2 1.4 %fusion = (f32[1,512]{1,0:T(1,128)}, f32[1,512]{1,0:T(1,128)}) fusion(f32[8,512]{1,0:T(8,128)} %get-tuple-element.29), kind=kLoop, calls=%fused_computation.9 | loop fusion | bytes 8192 | tf_op jit(solution)/shard_map/slice | solution.py:361
  14.6 0.8 %reverse = s32[2,1152]{1,0:T(2,128)S(1)} reverse(s32[2,1152]{1,0:T(2,128)S(1)} %bitcast.20), dimensions={1} | reverse | bytes 18432
  15.5 0.1 slice_bitcast_fusion.3
  15.6 0.1 slice_bitcast_fusion.2
  15.8 0.1 pad_add_fusion
  15.8 0.7 pad.4.ids_ref
  16.5 9.2 %states.1 = (bf16[4,1024,128]{2,1,0:T(8,128)(2,1)}, bf16[4,1024,512]{2,1,0:T(8,128)(2,1)}, bf16[4,1024,128]{2,1,0:T(8,128)(2,1)}, f32[4,16,16,512]{3,2,1,0:T(8,128)}, f32[8,24,256]{2,1,0:T(8,128)}) custom-call(s32[4,8,1024]{2,1,0:T(8,128)} %pad.4.ids_ref, bf16[256,256]{1,0:T(8,128)(2,1)} %constant.34.clone.tri_ref, ...), custom_call_target="tpu_custom_call" | custom-call | tf_op jit(solution)/shard_map/states/pallas_call | solution.py:379
  25.8 16.6 %carry.1.inc_ref = bf16[8,16,256]{2,1,0:T(8,128)(2,1)} custom-call(f32[8,24,256]{2,1,0:T(8,128)} %get-tuple-element.27.s_ref), custom_call_target="tpu_custom_call" | custom-call | tf_op jit(solution)/shard_map/carry/pallas_call | solution.py:404
  42.3 21.5 %outputs.1 = bf16[1024,512]{1,0:T(8,128)(2,1)} custom-call(bf16[4,1024,128]{2,1,0:T(8,128)(2,1)} %get-tuple-element.23.oh_ref, bf16[4,1024,512]{2,1,0:T(8,128)(2,1)} %get-tuple-element.24.x_ref, bf16[4,1024,128]{2,1,0:T(8,128)(2,1)} %get-tuple-element.25.kv_ref, f32[4,16,16,512]{3,2,1,0:T(8,128)} %get-tuple-element.26.sloc_ref, ...), custom_call_target="tpu_custom_call" | custom-call | tf_op jit(solution)/shard_map/outputs/pallas_call | solution.py:430
  63.8 2.1 %reshape.17 = bf16[1024,2,256]{2,1,0:T(2,128)(2,1)} reshape(bf16[1024,512]{1,0:T(8,128)(2,1)} %outputs.1) | data formatting | bytes 2097152 | tf_op jit(solution)/shard_map/reshape | solution.py:447
  (8 shorter events, 0.1 us)

commit v5 on v4

--- a/solution.py
+++ b/solution.py
@@ -27,12 +27,31 @@
     return jnp.dot(a, b, preferred_element_type=jnp.float32)
 
 
+def pack_log(log):
+    log = jnp.broadcast_to(log, (16, log.shape[1]))
+    row = lax.broadcasted_iota(jnp.int32, log.shape, 0)
+    hi = log.astype(jnp.bfloat16).astype(jnp.float32)
+    mid = (log - hi).astype(jnp.bfloat16).astype(jnp.float32)
+    picked = jnp.where(row == 0, hi, jnp.where(row == 1, mid, log - hi - mid))
+    return jnp.where(row < 3, picked, 0.0).astype(jnp.bfloat16)
+
+
+def unpack_log(rows):
+    return jnp.sum(rows.astype(jnp.float32), axis=0, keepdims=True)
+
+
 def logs_of(tri, oh, ld):
     counts = [dot(tri, oh[i : i + TRI]).astype(jnp.bfloat16) for i in range(0, ROWS, TRI)]
     return dot(jnp.concatenate(counts, axis=0), ld)
 
 
-def state_kernel_body(ids_ref, tri_ref, tx_ref, tst_ref, tdt_ref, ld_ref, oh_ref, x_ref, kv_ref, sloc_ref, sfin_ref, state_ref, log_ref):
+def state_kernel_body(chs, groups, ids_ref, tri_ref, tx_ref, tst_ref, tdt_ref, ld_ref, oh_ref, x_ref, kv_ref, sloc_ref, inc_ref, state_ref, log_ref, sfin_ref, *carry):
+    stream, step = pl.program_id(0), pl.program_id(1)
+
+    @pl.when((stream == 0) & (step == 0))
+    def _():
+        carry_body(chs, groups, True, sfin_ref, inc_ref, *carry)
+
     @pl.when(pl.program_id(1) == 0)
     def _():
         state_ref[...] = jnp.zeros_like(state_ref)
@@ -67,8 +86,12 @@
     log_ref[...] = log
     for i in range(2):
         lanes = slice(i * half, (i + 1) * half)
-        sfin_ref[i, 0:16, :] = state[:, lanes]
-        sfin_ref[i, 16:24, :] = jnp.broadcast_to(log[:, lanes], (8, half))
+        sfin_ref[stream * 2 + i, 0:16, :] = state[:, lanes].astype(jnp.bfloat16)
+        sfin_ref[stream * 2 + i, 16:32, :] = pack_log(log[:, lanes])
+
+    @pl.when((stream == pl.num_programs(0) - 1) & (step == pl.num_programs(1) - 1))
+    def _():
+        carry_body(chs, groups, False, sfin_ref, inc_ref, *carry)
 
 
 def output_kernel_body(
@@ -158,6 +181,27 @@
     own[...] = jnp.zeros_like(own)
     own[0, :wins, :] = tokens_ref[:, pl.ds(pl.multiple_of(ch * rows, 128), 128)]
     own[1, :wins, :] = tokens_ref[:, pl.ds(pl.multiple_of(ch * rows + rows - 128, 128), 128)]
+    def remote(src, dst, ssem, rsem, device):
+        return pltpu.make_async_remote_copy(
+            src_ref=src, dst_ref=dst, send_sem=ssem, recv_sem=rsem, device_id=device,
+            device_id_type=MESH,
+        )
+
+    def table_copies(d, slot):
+        return (
+            remote(packed, packed_all.at[slot], psend.at[d], precv.at[d], mate(d)),
+            remote(ow_ref, ow_all.at[slot], osend.at[d], orecv.at[d], mate(d)),
+        )
+
+    edge_copies = (
+        remote(own.at[1], edges.at[0], esend.at[0], erecv.at[0], after),
+        remote(own.at[0], edges.at[1], esend.at[1], erecv.at[1], before),
+    )
+    pl.semaphore_wait(barrier, 1 + chs)
+    for copy in edge_copies:
+        copy.start()
+    for d in range(1, chs):
+        table_copies(d, ch)[1].start()
     width, heads = iw_ref.shape[1], stw_ref.shape[0]
     emb = emb_ref[...]
     packed[...] = jnp.zeros_like(packed)
@@ -178,28 +222,8 @@
     packed[40:41, :] = skip[0:1]
     packed[41:42, :] = gain_ref[...]
 
-    def remote(src, dst, ssem, rsem, device):
-        return pltpu.make_async_remote_copy(
-            src_ref=src, dst_ref=dst, send_sem=ssem, recv_sem=rsem, device_id=device,
-            device_id_type=MESH,
-        )
-
-    def table_copies(d, slot):
-        return (
-            remote(packed, packed_all.at[slot], psend.at[d], precv.at[d], mate(d)),
-            remote(ow_ref, ow_all.at[slot], osend.at[d], orecv.at[d], mate(d)),
-        )
-
-    edge_copies = (
-        remote(own.at[1], edges.at[0], esend.at[0], erecv.at[0], after),
-        remote(own.at[0], edges.at[1], esend.at[1], erecv.at[1], before),
-    )
-    pl.semaphore_wait(barrier, 1 + chs)
     for d in range(1, chs):
-        for copy in table_copies(d, ch):
-            copy.start()
-    for copy in edge_copies:
-        copy.start()
+        table_copies(d, ch)[0].start()
     packed_all[ch] = packed[...]
     ow_all[ch] = ow_ref[...]
 
@@ -232,7 +256,7 @@
 
 
 def carry_body(
-    chs, groups, s_ref, out_ref, first, total, second, third, landed,
+    chs, groups, opening, s_ref, out_ref, first, total, second, third, landed,
     send1, recv1, send2, recv2, send3, recv3,
 ):
     me = lax.axis_index("seq") * chs + lax.axis_index("ch")
@@ -242,14 +266,16 @@
     mate = lambda d: place(g * GROUP + lax.rem(q + d, GROUP))
     peer = lambda d: place(lax.rem(g + d, groups) * GROUP + q)
     barrier = pltpu.get_barrier_semaphore()
-    for d in range(1, GROUP):
-        pl.semaphore_signal(barrier, inc=1, device_id=mate(d), device_id_type=MESH)
 
     def greet(d, _):
         pl.semaphore_signal(barrier, inc=1, device_id=peer(d), device_id_type=MESH)
         return 0
 
-    lax.fori_loop(1, groups, greet, 0)
+    if opening:
+        for d in range(1, GROUP):
+            pl.semaphore_signal(barrier, inc=1, device_id=mate(d), device_id_type=MESH)
+        lax.fori_loop(1, groups, greet, 0)
+        return
     pl.semaphore_wait(barrier, GROUP - 1 + groups - 1)
 
     def remote(src, dst, ssem, rsem, device):
@@ -272,14 +298,14 @@
     f32, bf16 = jnp.float32, jnp.bfloat16
     zero = jnp.zeros(out_ref.shape[1:], f32)
     member = lambda k: k + strand * (GROUP - 1 - 2 * k)
-    logs = [first[member(k), 16:17, :] for k in range(GROUP)]
+    logs = [unpack_log(first[member(k), 16:32, :]) for k in range(GROUP)]
     grow = [jnp.exp(log) for log in logs]
-    added = [first[member(k), 0:16, :] for k in range(GROUP)]
+    added = [first[member(k), 0:16, :].astype(f32) for k in range(GROUP)]
     state = zero
     for k in range(GROUP):
         state = grow[k] * state + added[k]
-    total[0:16, :] = state
-    total[16:24, :] = jnp.broadcast_to(sum(logs), (8, state.shape[1]))
+    total[0:16, :] = state.astype(bf16)
+    total[16:32, :] = pack_log(sum(logs))
 
     def across(d, slot):
         return remote(total, second.at[slot], send2.at[d], recv2.at[d], peer(d))
@@ -299,7 +325,7 @@
 
     def earlier(k, state):
         at = k + strand * (groups - 1 - 2 * k)
-        new = jnp.exp(second[at, 16:17, :]) * state + second[at, 0:16, :]
+        new = jnp.exp(unpack_log(second[at, 16:32, :])) * state + second[at, 0:16, :].astype(f32)
         return jnp.where(k < order, new, state)
 
     state = lax.fori_loop(0, groups, earlier, zero)
@@ -376,8 +402,10 @@
         (index[:, None] >= index[None]) & (index[:, None] // SUB == index[None] // SUB), bf16
     )
     row_spec = lambda n: pl.BlockSpec((1, ROWS, n), lambda s, b: (s, b, 0))
-    onehot, x, kv, sloc, sfin = pl.pallas_call(
-        state_kernel_body,
+    groups = devices // GROUP
+    piece, message = (16, full // 2), (32, full // 2)
+    onehot, x, kv, sloc, incoming = pl.pallas_call(
+        partial(state_kernel_body, chs, groups),
         grid=(streams, steps),
         in_specs=[pl.BlockSpec((1, 8, ROWS), lambda s, b: (s, 0, b))] + [whole_spec(v) for v in (tri, tx, tst, tdt, ld)],
         out_specs=[
@@ -385,38 +413,31 @@
             row_spec(full),
             row_spec(128),
             pl.BlockSpec((1, subs, 16, full), lambda s, b: (s, b, 0, 0)),
-            pl.BlockSpec((2, 24, full // 2), lambda s, b: (s, 0, 0)),
+            pl.BlockSpec((GROUP,) + piece, lambda s, b: (0, 0, 0)),
         ],
         out_shape=[
             jax.ShapeDtypeStruct((streams, rows, COLS), bf16),
             jax.ShapeDtypeStruct((streams, rows, full), bf16),
             jax.ShapeDtypeStruct((streams, rows, 128), bf16),
             jax.ShapeDtypeStruct((streams, steps * subs, 16, full), f32),
-            jax.ShapeDtypeStruct((streams * 2, 24, full // 2), f32),
+            jax.ShapeDtypeStruct((GROUP,) + piece, bf16),
         ],
-        scratch_shapes=[pltpu.VMEM((16, full), f32), pltpu.VMEM((1, full), f32)],
-        compiler_params=pltpu.CompilerParams(vmem_limit_bytes=56 << 20),
-        name="states",
-    )(taps, tri, tx, tst, tdt, ld)
-
-    groups = devices // GROUP
-    piece, message = (16, full // 2), (24, full // 2)
-    incoming = pl.pallas_call(
-        partial(carry_body, chs, groups),
-        in_specs=[vmem],
-        out_specs=vmem,
-        out_shape=jax.ShapeDtypeStruct((GROUP,) + piece, bf16),
         scratch_shapes=[
-            pltpu.VMEM((GROUP,) + message, f32),
-            pltpu.VMEM(message, f32),
-            pltpu.VMEM((groups,) + message, f32),
+            pltpu.VMEM((16, full), f32),
+            pltpu.VMEM((1, full), f32),
+            pltpu.VMEM((GROUP,) + message, bf16),
+            pltpu.VMEM((GROUP,) + message, bf16),
+            pltpu.VMEM(message, bf16),
+            pltpu.VMEM((groups,) + message, bf16),
             pltpu.VMEM((GROUP,) + piece, bf16),
             pltpu.VMEM((GROUP,) + piece, bf16),
         ]
         + [dma((GROUP,))] * 2 + [dma((groups,))] * 2 + [dma((GROUP,))] * 2,
-        compiler_params=pltpu.CompilerParams(collective_id=1, has_side_effects=True),
-        name="carry",
-    )(sfin)
+        compiler_params=pltpu.CompilerParams(
+            vmem_limit_bytes=56 << 20, collective_id=1, has_side_effects=True
+        ),
+        name="states",
+    )(taps, tri, tx, tst, tdt, ld)
 
     lane, t = np.arange(full)[None], np.arange(SUB)[:, None]
     causal = jnp.asarray(t >= lane % SUB, f32)

time: 66.4 us -> 62.6 us (0.943)
  Pallas kernels: 58.9 us -> 55.2 us
    pallas_call x2 -> x1, Pallas kernels: 25.8 us -> 22.1 us  [on_device(): pl.pallas_call(partial(state_kernel_body, chs, groups), grid=(streams, st...]
where the time goes in v5:
time: 62.6 us; the launch traced here: 62.2 us
  Pallas kernels  55.2 us (88%)
  local copies, waits for them, and re-layouts  6.06 us (10%)
  other arithmetic  0.84 us (1%)
    pallas_call x1, Pallas kernels, on_device(): pl.pallas_call(partial(state_kernel_body, chs, groups), grid=(streams, st...  22.1 us
    pallas_call x1, Pallas kernels, on_device(): pl.pallas_call(output_kernel_body, grid=(wins, 2, steps), in_specs=[strea...  21.4 us
    pallas_call x1, Pallas kernels, on_device(): pl.pallas_call(partial(exchange_body, chs, devices, rows), in_specs=[vmem...  11.7 us
    reshape x1, local copies, waits for them, and re-layouts, on_device(): return out.reshape(rows, wins, model)  2.13 us
    slice x1, local copies, waits for them, and re-layouts, on_device(): skip_all, gain_all = (vec[0:1], vec[1:2])  1.39 us

profile of v5, /device:TPU:0, one launch (start us, length us, event | category | flops | bytes accessed | tf_op | source)
XLA Modules:
  0.0 62.2 jit_solution(14236696406285613847)
XLA Ops:
  0.0 0.7 %constant_dynamic-slice_fusion = s32[2,1024]{1,0:T(2,128)S(1)} fusion(s32[2,2048]{1,0:T(2,128)} %tokens_ref.1, s32[]{:T(128)S(6)} %select_n.30), kind=kLoop, calls=%fused_computation.8 | loop fusion | bytes 16388 | tf_op jit(solution)/shard_map/dynamic_slice | solution.py:388
  0.7 11.7 %exchange.1 = (bf16[128,512]{1,0:T(8,128)(2,1)}, bf16[128,128]{1,0:T(8,128)(2,1)}, bf16[128,512]{1,0:T(8,128)(2,1)}, bf16[128,512]{1,0:T(8,128)(2,1)}, bf16[128,...) custom-call(s32[2,2048]{1,0:T(2,128)} %tokens_ref.1, ...), custom_call_target="tpu_custom_call" | custom-call | tf_op jit(solution)/shard_map/exchange/pallas_call | solution.py:363
  12.4 0.8 %select_bitcast_fusion = (s32[2,3]{1,0:T(2,128)S(1)}, s32[2,3]{1,0:T(2,128)S(1)}) fusion(s32[2,8,128]{2,1,0:T(8,128)} %get-tuple-element.18, pred[]{:T(512)S(6)} %lt.13, pred[]{:T(512)S(6)} %gt.3), kind=kLoop, calls=%fused_computation.6 | loop fusion | flops 12 | bytes 98 | tf_op jit(solution)/shard_map/jit(_where)/select_n | solution.py:391
  13.1 0.1 concatenate.3
  13.2 1.4 %fusion = (f32[1,512]{1,0:T(1,128)}, f32[1,512]{1,0:T(1,128)}) fusion(f32[8,512]{1,0:T(8,128)} %get-tuple-element.29), kind=kLoop, calls=%fused_computation.9 | loop fusion | bytes 8192 | tf_op jit(solution)/shard_map/slice | solution.py:387
  14.6 0.8 %reverse = s32[2,1152]{1,0:T(2,128)S(1)} reverse(s32[2,1152]{1,0:T(2,128)S(1)} %bitcast.20), dimensions={1} | reverse | bytes 18432
  15.5 0.1 slice_bitcast_fusion.3
  15.6 0.1 slice_bitcast_fusion.2
  15.8 0.1 pad_add_fusion
  15.8 0.7 %pad.4.ids_ref = s32[4,8,1024]{2,1,0:T(8,128)} pad(s32[4,4,1024]{2,1,0:T(4,128)S(1)} %pad_add_fusion, s32[]{:T(128)} %constant.11.clone.1), padding=0_0x0_4x0_0 | pad | bytes 196612 | tf_op jit(solution)/shard_map/jit(_pad)/pad | solution.py:396
  16.5 22.1 %states.1 = (bf16[4,1024,128]{2,1,0:T(8,128)(2,1)}, bf16[4,1024,512]{2,1,0:T(8,128)(2,1)}, bf16[4,1024,128]{2,1,0:T(8,128)(2,1)}, f32[4,16,16,512]{3,2,1,0:T(8,128)}, bf16[8,16,256]{2,1,0:T(8,128)(2,1)}) custom-call(s32[4,8,1024]{2,1,0:T(8,128)} %pad.4.ids_ref, bf16[256,256]{1,0:T(8,128)(2,1)} %constant.34.clone.tri_ref, ...), custom_call_target="tpu_custom_call" | custom-call | tf_op jit(solution)/shard_map/states/pallas_call | solution.py:407
  38.6 21.4 %outputs.1 = bf16[1024,512]{1,0:T(8,128)(2,1)} custom-call(bf16[4,1024,128]{2,1,0:T(8,128)(2,1)} %get-tuple-element.23.oh_ref, bf16[4,1024,512]{2,1,0:T(8,128)(2,1)} %get-tuple-element.24.x_ref, bf16[4,1024,128]{2,1,0:T(8,128)(2,1)} %get-tuple-element.25.kv_ref, f32[4,16,16,512]{3,2,1,0:T(8,128)} %get-tuple-element.26.sloc_ref, ...), custom_call_target="tpu_custom_call" | custom-call | tf_op jit(solution)/shard_map/outputs/pallas_call | solution.py:451
  60.0 2.1 %reshape.17 = bf16[1024,2,256]{2,1,0:T(2,128)(2,1)} reshape(bf16[1024,512]{1,0:T(8,128)(2,1)} %outputs.1) | data formatting | bytes 2097152 | tf_op jit(solution)/shard_map/reshape | solution.py:468
  (8 shorter events, 0.1 us)
